TPU v7x, 32 devices: a whole 2x2x4 slice. The times are simulated.
32 devices in a mesh: slab: 2 (over x), coarse: 8 (over z, y), fine: 2 (over core).
Axes of the slice: x: 2, y: 2, z: 4, core: 2. Of those that a mesh axis runs over, the one named last changes fastest.
Arguments:
- features: bfloat16 [196608, 256], P(('slab', 'coarse', 'fine')), parts along dimension 0, may hold values from -6 to 6
- weight: bfloat16 [256, 256], replicated, may hold values from -1.5 to 1.5
- bias_vector: float32 [256], replicated, may hold values from -3 to 3
- tile_nbrs: int32 [4, 1536], P(None, ('slab', 'coarse', 'fine')), parts along dimension 1, may hold values from 0 to 767, as said below
- nbr_local: int32 [16, 196608], P(None, ('slab', 'coarse', 'fine')), parts along dimension 1, may hold values from 0 to 511
- edge_count: int32 [16, 196608], P(None, ('slab', 'coarse', 'fine')), parts along dimension 1, may hold values from 1 to 3
- cotangent: bfloat16 [196608, 256], P(('slab', 'coarse', 'fine')), parts along dimension 0, may hold values from -6 to 6
Outputs:
- output: bfloat16 [196608, 256], P(('slab', 'coarse', 'fine')), parts along dimension 0
- grad_features: bfloat16 [196608, 256], P(('slab', 'coarse', 'fine')), parts along dimension 0
- grad_weight: float32 [512, 256], P('slab'), parts along dimension 0
- grad_bias: float32 [512], P('slab'), parts along dimension 0
There are 2 independent parts, one for each index of `slab`. A program takes and returns all parts, laid end to end along the dimension named above; an argument that names none is the same for every part. Nothing has to cross between parts.
Inputs may be any that keep to these rules, and one draw needn't show every extreme that they name: tile_nbrs[0, t] == t for every tile. For each device's tiles (aligned blocks of 48 tiles, owner of tile id u is u // 48), the slots 1 to 3 name tiles of any one other device at most 4 times, and exactly 4 times for at least one other device in every draw.
All inputs are finite; a program needn't handle non-finite values.
Results may differ from a plain program's by a relative error of at most 0.0069.
Values may be sent and summed in bfloat16 or wider, within the bound.
No kernel may reach another device: no remote copies, remote signals or barrier semaphores. Data moves between devices by JAX's collectives and lax.ppermute only.
A program may use at most 192 MiB of HBM per device.

v0:
```python
import math

import jax
import jax.numpy as jnp
from jax import lax
from jax.sharding import PartitionSpec as P

C = 256
TILE = 128
NB = 4


def compare_blocks(targets, portions, width):
    columns = jnp.arange(width, dtype=jnp.int32)
    matched = jnp.where(targets[..., None] == columns, portions[..., None], 0.0)
    return jnp.sum(matched, axis=1)


def edge_blocks(nbr_part, count_part):
    point_count = nbr_part.shape[1]
    counts_float = count_part.astype(jnp.float32)
    degree = jnp.sum(counts_float, axis=0)
    weights = counts_float / degree[None, :]
    dense_rows = compare_blocks(nbr_part[None], weights[None], NB * TILE)[0]
    return dense_rows.astype(jnp.bfloat16).reshape(point_count // TILE, TILE, NB * TILE)


def shards(features, weight, bias_vector, tile_nbrs, nbr_local, edge_count, cotangent):
    devices = lax.axis_size("coarse") * lax.axis_size("fine")
    position = lax.axis_index(("coarse", "fine"))
    tile_count = features.shape[0] // TILE
    capacity = max(1, (NB - 1) * tile_count // (2 * (devices - 1)))
    slots = devices * capacity
    x_tiles = features.reshape(tile_count, TILE, C)
    owners = tile_nbrs // tile_count
    within = tile_nbrs % tile_count
    remote = owners != position
    onehot = (
        (owners.reshape(-1)[:, None] == jnp.arange(devices, dtype=jnp.int32)[None, :])
        & remote.reshape(-1)[:, None]
    ).astype(jnp.int32)
    ranking = jnp.sum((jnp.cumsum(onehot, axis=0) - onehot) * onehot, axis=1).reshape(owners.shape)
    buffer_slot = jnp.where(remote, owners * capacity + ranking, slots)
    table_rows = jnp.where(remote, tile_count + buffer_slot, within)
    requests = (
        jnp.zeros((slots,), jnp.int32)
        .at[buffer_slot.reshape(-1)]
        .set(within.reshape(-1), mode="drop")
        .reshape(devices, capacity)
    )
    wanted = lax.all_to_all(
        requests, ("coarse", "fine"), split_axis=0, concat_axis=0, tiled=True
    ).reshape(-1)
    outgoing = x_tiles[wanted].reshape(devices, capacity, TILE, C)
    arrived = lax.all_to_all(outgoing, ("coarse", "fine"), split_axis=0, concat_axis=0, tiled=True)
    tile_table = jnp.concatenate([x_tiles, arrived.reshape(slots, TILE, C)], axis=0)
    nearby = tile_table[table_rows.T].reshape(tile_count, NB * TILE, C)
    blocks = edge_blocks(nbr_local, edge_count)
    aggregated = jnp.einsum("tij,tjc->tic", blocks, nearby, preferred_element_type=jnp.float32)
    aggregated = aggregated.astype(jnp.bfloat16).reshape(-1, C)
    preact = jnp.dot(aggregated, weight, preferred_element_type=jnp.float32) + bias_vector
    sigma = jax.nn.sigmoid(preact)
    output = (preact * sigma).astype(jnp.bfloat16)
    slope = sigma * (1.0 + preact * (1.0 - sigma))
    preact_grad = (cotangent.astype(jnp.float32) * slope).astype(jnp.bfloat16)
    weight_part = lax.dot_general(
        aggregated, preact_grad, (((0,), (0,)), ((), ())), preferred_element_type=jnp.float32
    )
    bias_part = jnp.sum(preact_grad.astype(jnp.float32), axis=0)
    weight_sum, bias_sum = lax.psum((weight_part, bias_part), ("coarse", "fine"))
    normalizer = 1.0 / math.sqrt(features.shape[0] * devices)
    gradient = lax.dot_general(
        preact_grad, weight, (((1,), (1,)), ((), ())), preferred_element_type=jnp.float32
    ).astype(jnp.bfloat16)
    gradient = gradient.reshape(tile_count, TILE, C)
    backward = jnp.einsum("tij,tic->tjc", blocks, gradient, preferred_element_type=jnp.float32)
    backward = backward.reshape(tile_count, NB, TILE, C)
    own_terms = backward[:, 0]
    other_terms = backward[:, 1:]
    accumulated = (
        jnp.zeros((tile_count + slots, TILE, C), jnp.float32).at[table_rows[1:].T].add(other_terms)
    )
    returned = lax.all_to_all(
        accumulated[tile_count:].reshape(devices, capacity, TILE, C).astype(jnp.bfloat16),
        ("coarse", "fine"),
        split_axis=0,
        concat_axis=0,
        tiled=True,
    ).astype(jnp.float32)
    summed = (accumulated[:tile_count] + own_terms).at[wanted].add(returned.reshape(slots, TILE, C))
    grad_features = summed.reshape(-1, C).astype(jnp.bfloat16)
    return (output, grad_features, weight_sum * normalizer, bias_sum * normalizer)


def solution(mesh):
    return jax.shard_map(
        shards,
        mesh=mesh,
        in_specs=(
            P(("slab", "coarse", "fine"), None),
            P(),
            P(),
            P(None, ("slab", "coarse", "fine")),
            P(None, ("slab", "coarse", "fine")),
            P(None, ("slab", "coarse", "fine")),
            P(("slab", "coarse", "fine"), None),
        ),
        out_specs=(
            P(("slab", "coarse", "fine"), None),
            P(("slab", "coarse", "fine"), None),
            P("slab", None),
            P("slab"),
        ),
        check_vma=False,
    )
```

profile of v0, /device:TPU:0, one launch (start us, length us, event | category | flops | bytes accessed | tf_op | source)
XLA Modules:
  0.0 437.7 jit_solution(3613226867180488434)
XLA Ops:
  7.2 0.0 copy-start
  7.2 0.7 add_select_fusion
  7.9 0.1 reshape.188
  8.0 0.7 broadcast_compare_fusion
  8.7 0.1 and.26
  8.8 0.1 eq.48
  8.9 0.6 reduce-window.6
  9.5 0.2 slice_reduce_fusion
  9.7 0.1 bitcast_bitcast_fusion
  9.8 0.1 reshape.153
  9.9 0.7 compare_select_fusion.2
  10.6 0.1 reshape.154
  10.7 1.2 scatter_custom_fusion
  11.9 0.1 all_to_all.12
  12.0 13.6 %all_to_all.19 = s32[16,1,4]{2,1,0:T(1,128)S(1)} all-to-all(s32[16,1,4]{2,1,0:T(1,128)S(1)} %bitcast.63), channel_id=1, replica_groups=mesh['slab'=2,'coarse'=8,'fine'=2] {'coarse','fine'}, dimensions={0} | all-to-all | bytes 512 | tf_op jit(solution)/shard_map/all_to_all | solution.py:51
  25.6 0.5 broadcast.113
  26.1 0.7 reduce.6
  26.8 0.1 reshape.156
  26.9 4.6 %gather_fusion = bf16[64,128,256]{2,1,0:T(8,128)(2,1)} fusion(bf16[48,128,256]{2,1,0:T(8,128)(2,1)} %bitcast.56, s32[1024]{0:T(1024)S(1)} %pad_clamp_fusion.1), kind=kCustom, calls=%fused_computation | custom fusion | bytes 8388864 | tf_op jit(solution)/shard_map/gather | solution.py:54
  31.6 4.6 %all-to-all-start.1 = ((bf16[16,4,128,256]{3,2,1,0:T(8,128)(2,1)}), bf16[16,4,128,256]{3,2,1,0:T(8,128)(2,1)}, u32[]{:S(2)}, u32[]{:S(2)}) async-start(bf16[16,4,128,256]{3,2,1,0:T(8,128)(2,1)} %bitcast.59), calls=%async_computation.1 | async-start | bytes 8388608 | tf_op jit(solution)/shard_map/all_to_all | solution.py:55
  36.1 0.0 copy-start.2
  36.2 0.1 copy.27
  36.2 0.1 reshape.194
  36.4 0.1 copy.26
  36.5 0.1 reshape.178
  36.6 1.3 convert_reduce_fusion.1
  37.9 1.0 convert_divide_fusion
  38.9 40.4 %select_reduce_fusion = bf16[6144,512]{1,0:T(8,128)(2,1)} fusion(f32[16,6144]{1,0:T(8,128)S(1)} %convert_divide_fusion, s32[16,6144]{1,0:T(8,128)} %param.11), kind=kLoop, calls=%fused_computation.5 | loop fusion | flops 147849216 | bytes 7077888 | tf_op jit(solution)/shard_map/reduce_sum | solution.py:16
  79.3 34.3 %all-to-all-done.1 = bf16[16,4,128,256]{3,2,1,0:T(8,128)(2,1)} async-done(((bf16[16,4,128,256]{3,2,1,0:T(8,128)(2,1)}), bf16[16,4,128,256]{3,2,1,0:T(8,128)(2,1)}, u32[]{:S(2)}, u32[]{:S(2)}) %all-to-all-start.1) | async-done | bytes 4194336 | tf_op jit(solution)/shard_map/all_to_all | solution.py:55
  113.6 0.0 copy-done.2
  113.6 5.7 %pad_maximum_fusion = bf16[112,128,256]{2,1,0:T(8,128)(2,1)} fusion(bf16[64,128,256]{2,1,0:T(8,128)(2,1)} %bitcast.7, bf16[48,128,256]{2,1,0:T(8,128)(2,1)S(1)} %bitcast.57), kind=kLoop, calls=%fused_computation.10 | loop fusion | flops 3670016 | bytes 14680064 | tf_op jit(solution)/shard_map/concatenate | solution.py:56
  119.3 11.3 %gather_fusion.1 = bf16[192,128,256]{2,1,0:T(8,128)(2,1)} fusion(bf16[112,128,256]{2,1,0:T(8,128)(2,1)} %pad_maximum_fusion, s32[1024]{0:T(1024)S(1)} %pad_clamp_fusion), kind=kCustom, calls=%fused_computation.1 | custom fusion | bytes 25166592 | tf_op jit(solution)/shard_map/gather | solution.py:57
  130.7 0.0 copy-start.6
  130.7 0.0 copy-start.7
  130.7 8.3 %convolution_convert_fusion.1 = bf16[48,128,256]{2,1,0:T(8,128)(2,1)S(1)} fusion(bf16[48,128,512]{2,1,0:T(8,128)(2,1)} %bitcast.52, bf16[48,512,256]{2,1,0:T(8,128)(2,1)} %bitcast.51), kind=kOutput, calls=%fused_computation.18 | convolution fusion | flops 1612185600 | bytes 22020096 | tf_op jit(solution)/shard_map/tij,tjc->tic/dot_general | solution.py:59
  139.0 0.0 copy-start.3
  139.0 0.0 copy-done
  139.0 0.0 copy-done.6
  139.1 0.0 copy-done.7
  139.1 4.6 %convert_reduce_fusion = (f32[256]{0:T(256)S(1)}, bf16[6144,256]{1,0:T(8,128)(2,1)S(1)}, bf16[6144,256]{1,0:T(8,128)(2,1)}) fusion(bf16[6144,256]{1,0:T(8,128)(2,1)S(1)} %copy-done.6, f32[256]{0:T(256)S(1)} %copy-done.7, bf16[6144,256]{1,0:T(8,128)(2,1)S(1)} %bitcast.60, bf16[256,256]{1,0:T(8,128)(2,1)S(1)} %copy-done), kind=kOutput, calls=%fused_computation.13 | convolution fusion | flops 828899072 | bytes 12716032 | tf_op jit(solution)/shard_map/dot_general | solution.py:61
  143.7 0.0 copy-done.3
  143.7 1.7 copy-done.5
  145.3 1.0 convolution_convert_fusion
  146.3 14.6 %fusion.9 = f32[48,512,256]{2,1,0:T(8,128)} fusion(bf16[48,128,512]{2,1,0:T(8,128)(2,1)} %bitcast.53, bf16[48,128,256]{2,1,0:T(8,128)(2,1)S(1)} %bitcast.55), kind=kOutput, calls=%fused_computation.52 | convolution fusion | flops 1610612736 | bytes 34603008 | tf_op jit(solution)/shard_map/tij,tic->tjc/dot_general | solution.py:76
  160.9 12.8 %slice.39 = f32[48,3,128,256]{3,2,1,0:T(8,128)} slice(f32[48,4,128,256]{3,2,1,0:T(8,128)} %bitcast.49), slice={[0:48], [1:4], [0:128], [0:256]} | slice | bytes 37748736 | tf_op jit(solution)/shard_map/slice | solution.py:79
  173.7 6.9 %broadcast_in_dim.36 = f32[112,128,256]{2,1,0:T(8,128)} broadcast(f32[]{:T(128)} %constant.17.clone.1), dimensions={} | broadcast | bytes 14680068 | tf_op jit(solution)/shard_map/broadcast_in_dim | solution.py:81
  180.6 43.3 %scatter_fusion = f32[112,128,256]{2,1,0:T(8,128)} fusion(f32[112,128,256]{2,1,0:T(8,128)} %broadcast_in_dim.36, s32[144]{0:T(256)S(1)} %reshape.194, f32[144,128,256]{2,1,0:T(8,128)} %bitcast.54), kind=kCustom, calls=%fused_computation.3 | custom fusion | flops 4718592 | bytes 56623680 | tf_op jit(solution)/shard_map/scatter-add | solution.py:81
  223.9 6.0 %slice.55 = bf16[64,128,256]{2,1,0:T(8,128)(2,1)} slice(f32[112,128,256]{2,1,0:T(8,128)} %scatter_fusion), slice={[48:112], [0:128], [0:256]} | slice | bytes 8388608 | tf_op jit(solution)/shard_map/slice | solution.py:84
  229.9 0.0 copy-start.4
  229.9 20.0 %all-to-all-start.2 = ((bf16[16,4,128,256]{3,2,1,0:T(8,128)(2,1)}), bf16[16,4,128,256]{3,2,1,0:T(8,128)(2,1)}, u32[]{:S(2)}, u32[]{:S(2)}) async-start(bf16[16,4,128,256]{3,2,1,0:T(8,128)(2,1)} %bitcast.58), calls=%async_computation.2 | async-start | bytes 8388608 | tf_op jit(solution)/shard_map/all_to_all | solution.py:83
  249.9 0.0 all-reduce.3.cloned.1.call-start
  250.0 0.0 copy-done.4
  250.0 3.6 fusion.10
  253.6 0.0 all-reduce.3.cloned.1.call-update
  253.6 94.5 %psum.15 = f32[256]{0:T(256)S(1)} all-reduce(f32[256]{0:T(256)S(1)} %get-tuple-element.4), channel_id=1, replica_groups=mesh['slab'=2,'coarse'=8,'fine'=2] {'coarse','fine'}, use_global_device_ids=true, to_apply=%region_10.11 | all-reduce | flops 256 | bytes 2048 | tf_op jit(solution)/shard_map/psum | solution.py:70
  348.1 8.7 %fusion = f32[48,128,256]{2,1,0:T(8,128)} fusion(f32[48,4,128,256]{3,2,1,0:T(8,128)} %bitcast.50, f32[112,128,256]{2,1,0:T(8,128)} %scatter_fusion), kind=kLoop, calls=%fused_computation.12 | loop fusion | flops 1572864 | bytes 18874368 | tf_op jit(solution)/shard_map/add | solution.py:90
  356.9 0.6 broadcast_multiply_fusion.1
  357.4 41.4 %all-reduce.3.cloned.1.call-done = f32[256,256]{1,0:T(8,128)} async-done(((f32[256,256]{1,0:T(8,128)}), f32[256,256]{1,0:T(8,128)}) %all-reduce.3.cloned.1.call-update) | async-done | bytes 262160 | tf_op jit(solution)/shard_map/psum | solution.py:70
  398.8 1.7 broadcast_multiply_fusion
  400.5 0.0 all-to-all-done.2
  400.5 6.5 %bitcast_convert_fusion = f32[64,128,256]{2,1,0:T(8,128)} fusion(bf16[16,4,128,256]{3,2,1,0:T(8,128)(2,1)} %all-to-all-done.2), kind=kLoop, calls=%fused_computation.17 | loop fusion | flops 2097152 | bytes 12582912 | tf_op jit(solution)/shard_map/reshape | solution.py:90
  407.1 18.9 %scatter_fusion.1 = f32[48,128,256]{2,1,0:T(8,128)} fusion(f32[48,128,256]{2,1,0:T(8,128)} %fusion, s32[64]{0:T(128)S(1)} %fusion.6, f32[64,128,256]{2,1,0:T(8,128)} %bitcast_convert_fusion), kind=kCustom, calls=%fused_computation.4 | custom fusion | flops 2097152 | bytes 25166080 | tf_op jit(solution)/shard_map/scatter-add | solution.py:90
  426.0 4.9 %convert_element_type.53 = bf16[48,128,256]{2,1,0:T(8,128)(2,1)} convert(f32[48,128,256]{2,1,0:T(8,128)} %scatter_fusion.1) | non-fusion elementwise | flops 1572864 | bytes 9437184 | tf_op jit(solution)/shard_map/convert_element_type | solution.py:91
  430.9 0.0 copy-done.1
  (12 shorter events, 0.1 us)
Async XLA Ops:
  7.2 131.9 %copy-start = (bf16[256,256]{1,0:T(8,128)(2,1)S(1)}, bf16[256,256]{1,0:T(8,128)(2,1)}, u32[]{:S(2)}) copy-start(bf16[256,256]{1,0:T(8,128)(2,1)} %param.8) | copy-start | bytes 393220
  31.6 82.0 %all-to-all-start.1 = ((bf16[16,4,128,256]{3,2,1,0:T(8,128)(2,1)}), bf16[16,4,128,256]{3,2,1,0:T(8,128)(2,1)}, u32[]{:S(2)}, u32[]{:S(2)}) async-start(bf16[16,4,128,256]{3,2,1,0:T(8,128)(2,1)} %bitcast.59), calls=%async_computation.1 | async-start | bytes 8388608 | tf_op jit(solution)/shard_map/all_to_all | solution.py:55
  36.1 77.5 %copy-start.2 = (bf16[6144,256]{1,0:T(8,128)(2,1)S(1)}, bf16[6144,256]{1,0:T(8,128)(2,1)}, u32[]{:S(2)}) copy-start(bf16[6144,256]{1,0:T(8,128)(2,1)} %param.7) | copy-start | bytes 9437188
  130.7 8.4 %copy-start.6 = (bf16[6144,256]{1,0:T(8,128)(2,1)S(1)}, bf16[6144,256]{1,0:T(8,128)(2,1)}, u32[]{:S(2)}) copy-start(bf16[6144,256]{1,0:T(8,128)(2,1)} %param.13) | copy-start | bytes 9437188
  130.7 8.4 %copy-start.7 = (f32[256]{0:T(256)S(1)}, f32[256]{0:T(256)}, u32[]{:S(2)}) copy-start(f32[256]{0:T(256)} %param.9) | copy-start | bytes 3076
  139.0 4.6 %copy-start.3 = (bf16[48,128,256]{2,1,0:T(8,128)(2,1)}, bf16[48,128,256]{2,1,0:T(8,128)(2,1)S(1)}, u32[]{:S(2)}) copy-start(bf16[48,128,256]{2,1,0:T(8,128)(2,1)S(1)} %convolution_convert_fusion.1) | copy-start | bytes 9437188
  143.7 1.7 copy-start.5
  229.9 20.1 %copy-start.4 = (bf16[48,128,256]{2,1,0:T(8,128)(2,1)S(1)}, bf16[48,128,256]{2,1,0:T(8,128)(2,1)}, u32[]{:S(2)}) copy-start(bf16[48,128,256]{2,1,0:T(8,128)(2,1)} %copy-done.3) | copy-start | bytes 9437188
  229.9 170.6 %all-to-all-start.2 = ((bf16[16,4,128,256]{3,2,1,0:T(8,128)(2,1)}), bf16[16,4,128,256]{3,2,1,0:T(8,128)(2,1)}, u32[]{:S(2)}, u32[]{:S(2)}) async-start(bf16[16,4,128,256]{3,2,1,0:T(8,128)(2,1)} %bitcast.58), calls=%async_computation.2 | async-start | bytes 8388608 | tf_op jit(solution)/shard_map/all_to_all | solution.py:83
  249.9 148.9 %all-reduce.3.cloned.1.call-start = ((), (), s32[]{:S(2)}) async-start(), calls=%async_computation.3 | async-start | bytes 524288 | tf_op jit(solution)/shard_map/psum | solution.py:70
  407.1 23.8 %copy-start.1 = (bf16[256,256]{1,0:T(8,128)(2,1)S(1)}, bf16[256,256]{1,0:T(8,128)(2,1)}, u32[]{:S(2)}) copy-start(bf16[256,256]{1,0:T(8,128)(2,1)} %param.8) | copy-start | bytes 393220
Sparse Core Ops, SparseCore 0:
  254.7 144.1 all-reduce.2
where the time goes:
time: 439 us; the launch traced here: 438 us
  other arithmetic  137 us (31%)
  blocking collectives  108 us (25%)
  waiting for transfers between devices  75.8 us (17%)
  local copies, waits for them, and re-layouts  46.2 us (11%)
  matrix products  32.1 us (7%)
  starting transfers between devices  24.6 us (6%)
  between operations  14.2 us (3%)
    psum x1, blocking collectives, shards(): lax.psum((weight_part, bias_part), ('coarse', 'fine'))  94.5 us
    scatter-add x1, other arithmetic, shards(): jnp.zeros((tile_count + slots, TILE, C), jnp.float32).at[table_rows[1:].T]  43.3 us
    psum x1, waiting for transfers between devices, shards(): lax.psum((weight_part, bias_part), ('coarse', 'fine'))  41.4 us
    reduce_sum x1, other arithmetic, compare_blocks(): return jnp.sum(matched, axis=1)  40.4 us
    all_to_all x1, waiting for transfers between devices, shards(): lax.all_to_all(outgoing, ('coarse', 'fine'), split_axis=0, concat_axis=0,...  34.3 us
    all_to_all x1, starting transfers between devices, shards(): lax.all_to_all(accumulated[tile_count:].reshape(devices, capacity, TILE,...  20 us
    scatter-add x1, other arithmetic, shards(): (accumulated[:tile_count] + own_terms).at[wanted]  18.9 us
    dot_general x1, matrix products, shards(): jnp.einsum('tij,tic->tjc', blocks, gradient, preferred_element_type=jnp.f...  14.6 us
  transfers between devices with their start and end apart: 3, of which 2 were waited for; matrix products, arithmetic and copies ran while one was open for 13% of the time, Pallas kernels for 0%

commit v1 on v0

v1 whole, which is shorter than its diff:
```python
import math

import jax
import jax.numpy as jnp
from jax import lax
from jax.experimental import pallas as pl
from jax.experimental.pallas import tpu as pltpu
from jax.sharding import PartitionSpec as P

C = 256
TILE = 128
NB = 4
GROUP = ("coarse", "fine")
VMEM = pltpu.MemorySpace.VMEM
SMEM = pltpu.MemorySpace.SMEM


def whole(space=VMEM):
    return pl.BlockSpec(memory_space=space)


def pack_kernel(position_ref, table_ref, x_ref, packed_ref, wanted_ref, wanted_s, table_sem, sems):
    devices, slot_count = table_ref.shape
    tile_count = x_ref.shape[0]
    capacity = packed_ref.shape[0] // devices
    position = position_ref[0]
    within = table_ref[...] - position * tile_count
    asker = lax.broadcasted_iota(jnp.int32, within.shape, 0)
    mine = (within >= 0) & (within < tile_count) & (asker != position)
    ones = jnp.where(mine, 1.0, 0.0)
    earlier = lax.broadcasted_iota(jnp.int32, (slot_count, slot_count), 0)
    later = lax.broadcasted_iota(jnp.int32, (slot_count, slot_count), 1)
    before = jnp.where(earlier < later, 1.0, 0.0).astype(jnp.bfloat16)
    ranking = jnp.dot(ones.astype(jnp.bfloat16), before, preferred_element_type=jnp.float32)
    lane = lax.broadcasted_iota(jnp.int32, wanted_ref.shape, 1)
    wanted = jnp.full(wanted_ref.shape, -1, jnp.int32)
    for rank in range(capacity):
        chosen = jnp.where(mine & (ranking.astype(jnp.int32) == rank), within + 1, 0)
        found = jnp.sum(chosen.astype(jnp.float32), axis=1, keepdims=True).astype(jnp.int32) - 1
        wanted = jnp.where(lane == rank, found, wanted)
    wanted_ref[...] = wanted
    copy = pltpu.make_async_copy(wanted_ref, wanted_s, table_sem)
    copy.start()
    copy.wait()
    for device in range(devices):
        for rank in range(capacity):
            tile = wanted_s[device, rank]

            @pl.when(tile >= 0)
            def _():
                slot = device * capacity + rank
                pltpu.make_async_copy(x_ref.at[tile], packed_ref.at[slot], sems.at[slot]).start()

    for device in range(devices):
        for rank in range(capacity):
            tile = wanted_s[device, rank]

            @pl.when(tile >= 0)
            def _():
                slot = device * capacity + rank
                pltpu.make_async_copy(x_ref.at[tile], packed_ref.at[slot], sems.at[slot]).wait()


def pack(position, table, x_tiles, capacity):
    devices = table.shape[0]
    return pl.pallas_call(
        pack_kernel,
        name="pack",
        in_specs=[whole(SMEM), whole(), whole()],
        out_specs=[pl.BlockSpec(memory_space=pl.ANY), whole()],
        out_shape=[
            jax.ShapeDtypeStruct((devices * capacity, TILE, C), jnp.bfloat16),
            jax.ShapeDtypeStruct((devices, 128), jnp.int32),
        ],
        scratch_shapes=[
            pltpu.SMEM((devices, 128), jnp.int32),
            pltpu.SemaphoreType.DMA,
            pltpu.SemaphoreType.DMA((devices * capacity,)),
        ],
        compiler_params=pltpu.CompilerParams(vmem_limit_bytes=16 << 20),
    )(position, table, x_tiles)


def blocks_kernel(nbr_ref, count_ref, rows_ref, columns_ref):
    counts = count_ref[...].astype(jnp.float32)
    weights = counts / jnp.sum(counts, axis=0, keepdims=True)
    targets = nbr_ref[...]
    for slot in range(NB):
        local = lax.broadcasted_iota(jnp.int32, (TILE, TILE), 0) + slot * TILE
        total = jnp.zeros((TILE, TILE), jnp.float32)
        for k in range(targets.shape[0]):
            total += jnp.where(targets[k : k + 1] == local, weights[k : k + 1], 0.0)
        columns_ref[0, slot] = total.astype(jnp.bfloat16)
        rows_ref[0, :, slot * TILE : (slot + 1) * TILE] = total.T.astype(jnp.bfloat16)


def build_blocks(nbr, count):
    entries, points = nbr.shape
    tile_count = points // TILE
    return pl.pallas_call(
        blocks_kernel,
        name="blocks",
        grid=(tile_count,),
        in_specs=[pl.BlockSpec((entries, TILE), lambda t: (0, t))] * 2,
        out_specs=[
            pl.BlockSpec((1, TILE, NB * TILE), lambda t: (t, 0, 0)),
            pl.BlockSpec((1, NB, TILE, TILE), lambda t: (t, 0, 0, 0)),
        ],
        out_shape=[
            jax.ShapeDtypeStruct((tile_count, TILE, NB * TILE), jnp.bfloat16),
            jax.ShapeDtypeStruct((tile_count, NB, TILE, TILE), jnp.bfloat16),
        ],
        compiler_params=pltpu.CompilerParams(vmem_limit_bytes=8 << 20),
    )(nbr, count)


def middle_kernel(
    rows_index, term_tile, term_slot, rows_ref, columns_ref, x_ref, arrived_ref, weight_ref, bias_ref, cot_ref,
    out_ref, agg_ref, pg_ref, grad_ref, terms_ref, near, terms, near_sems, sems,
):
    tile_count = x_ref.shape[0]
    slots = arrived_ref.shape[0]
    own = pltpu.make_async_copy(x_ref, near.at[pl.ds(0, tile_count)], near_sems.at[0])
    others = pltpu.make_async_copy(arrived_ref, near.at[pl.ds(tile_count, slots)], near_sems.at[1])
    own.start()
    others.start()
    own.wait()
    others.wait()
    weight = weight_ref[...]
    bias = bias_ref[...]

    def tile_step(t, carry):
        rows = rows_ref[t]
        first = jnp.concatenate([near[t], near[rows_index[1, t]]], axis=0)
        second = jnp.concatenate([near[rows_index[2, t]], near[rows_index[3, t]]], axis=0)
        total = jnp.dot(rows[:, : 2 * TILE], first, preferred_element_type=jnp.float32)
        total += jnp.dot(rows[:, 2 * TILE :], second, preferred_element_type=jnp.float32)
        aggregated = total.astype(jnp.bfloat16)
        agg_ref[t] = aggregated
        preact = jnp.dot(aggregated, weight, preferred_element_type=jnp.float32) + bias
        sigma = jax.nn.sigmoid(preact)
        out_ref[t] = (preact * sigma).astype(jnp.bfloat16)
        slope = sigma * (1.0 + preact * (1.0 - sigma))
        preact_grad = (cot_ref[t].astype(jnp.float32) * slope).astype(jnp.bfloat16)
        pg_ref[t] = preact_grad
        grad_ref[t] = lax.dot_general(
            preact_grad, weight, (((1,), (1,)), ((), ())), preferred_element_type=jnp.float32
        ).astype(jnp.bfloat16)
        return carry

    lax.fori_loop(0, tile_count, tile_step, 0)

    per = slots // sems.shape[0]

    def term_step(device, carry):
        for rank in range(per):
            slot = device * per + rank
            t = term_tile[slot]
            terms[slot] = jnp.dot(
                columns_ref[t, term_slot[slot]], grad_ref[t], preferred_element_type=jnp.float32
            ).astype(jnp.bfloat16)
        part = pl.ds(device * per, per)
        pltpu.make_async_copy(terms.at[part], terms_ref.at[part], sems.at[device]).start()
        return carry

    lax.fori_loop(0, sems.shape[0], term_step, 0)

    def finish(device, carry):
        part = pl.ds(device * per, per)
        pltpu.make_async_copy(terms.at[part], terms_ref.at[part], sems.at[device]).wait()
        return carry

    lax.fori_loop(0, sems.shape[0], finish, 0)


def middle(rows_index, term_tile, term_slot, rows, columns, x_tiles, arrived, weight, bias, cot, devices):
    tile_count = x_tiles.shape[0]
    slots = arrived.shape[0]
    tiles = jax.ShapeDtypeStruct((tile_count, TILE, C), jnp.bfloat16)
    return pl.pallas_call(
        middle_kernel,
        name="middle",
        in_specs=[whole(SMEM)] * 3 + [whole()] * 3 + [pl.BlockSpec(memory_space=pl.ANY)] + [whole()] * 3,
        out_specs=[whole()] * 4 + [pl.BlockSpec(memory_space=pl.ANY)],
        out_shape=[tiles] * 4 + [jax.ShapeDtypeStruct((slots, TILE, C), jnp.bfloat16)],
        scratch_shapes=[
            pltpu.VMEM((tile_count + slots, TILE, C), jnp.bfloat16),
            pltpu.VMEM((slots, TILE, C), jnp.bfloat16),
            pltpu.SemaphoreType.DMA((2,)),
            pltpu.SemaphoreType.DMA((devices,)),
        ],
        compiler_params=pltpu.CompilerParams(vmem_limit_bytes=58 << 20),
    )(rows_index, term_tile, term_slot, rows, columns, x_tiles, arrived, weight, bias, cot)


def local_kernel(target_ref, columns_ref, grad_ref, total_ref):
    tile_count = grad_ref.shape[0]

    def own_step(t, carry):
        total_ref[t] = jnp.dot(columns_ref[t, 0], grad_ref[t], preferred_element_type=jnp.float32)
        return carry

    lax.fori_loop(0, tile_count, own_step, 0)

    def other_step(t, carry):
        for slot in range(1, NB):
            target = target_ref[slot, t]

            @pl.when(target < tile_count)
            def _():
                total_ref[target] += jnp.dot(
                    columns_ref[t, slot], grad_ref[t], preferred_element_type=jnp.float32
                )

        return carry

    lax.fori_loop(0, tile_count, other_step, 0)


def local_terms(rows_index, columns, grad):
    return pl.pallas_call(
        local_kernel,
        name="local_terms",
        in_specs=[whole(SMEM), whole(), whole()],
        out_specs=whole(),
        out_shape=jax.ShapeDtypeStruct(grad.shape, jnp.float32),
        compiler_params=pltpu.CompilerParams(vmem_limit_bytes=24 << 20),
    )(rows_index, columns, grad)


def final_kernel(wanted_ref, local_ref, returned_ref, out_ref, total, returned, total_sem, sems):
    tile_count = local_ref.shape[0]
    devices = sems.shape[0]
    per = returned_ref.shape[0] // devices
    first = pltpu.make_async_copy(local_ref, total, total_sem)
    first.start()
    copies = []
    for device in range(devices):
        part = pl.ds(device * per, per)
        copies.append(pltpu.make_async_copy(returned_ref.at[part], returned.at[part], sems.at[device]))
        copies[-1].start()
    first.wait()
    for device in range(devices):
        copies[device].wait()
        for rank in range(per):
            target = wanted_ref[device, rank]

            @pl.when(target >= 0)
            def _():
                total[target] += returned[device * per + rank].astype(jnp.float32)

    def round_step(t, carry):
        out_ref[t] = total[t].astype(jnp.bfloat16)
        return carry

    lax.fori_loop(0, tile_count, round_step, 0)


def final_sum(wanted, local, returned, devices):
    return pl.pallas_call(
        final_kernel,
        name="final_sum",
        in_specs=[whole(SMEM), pl.BlockSpec(memory_space=pl.ANY), pl.BlockSpec(memory_space=pl.ANY)],
        out_specs=whole(),
        out_shape=jax.ShapeDtypeStruct(local.shape, jnp.bfloat16),
        scratch_shapes=[
            pltpu.VMEM(local.shape, jnp.float32),
            pltpu.VMEM(returned.shape, jnp.bfloat16),
            pltpu.SemaphoreType.DMA,
            pltpu.SemaphoreType.DMA((devices,)),
        ],
        compiler_params=pltpu.CompilerParams(vmem_limit_bytes=24 << 20),
    )(wanted, local, returned)


def exchange(array, devices):
    parted = array.reshape((devices, array.shape[0] // devices) + array.shape[1:])
    return lax.all_to_all(parted, GROUP, split_axis=0, concat_axis=0, tiled=True).reshape(array.shape)


def group_sum(part, devices, position):
    bits = devices.bit_length() - 1
    for bit in range(bits):
        half = part.shape[0] // 2
        upper = (position >> bit) & 1 == 1
        pairs = [(d, d ^ (1 << bit)) for d in range(devices)]
        sent = jnp.where(upper, part[:half], part[half:])
        kept = jnp.where(upper, part[half:], part[:half])
        part = kept + lax.ppermute(sent, GROUP, pairs)
    for bit in reversed(range(bits)):
        upper = (position >> bit) & 1 == 1
        pairs = [(d, d ^ (1 << bit)) for d in range(devices)]
        other = lax.ppermute(part, GROUP, pairs)
        part = jnp.where(upper, jnp.concatenate([other, part]), jnp.concatenate([part, other]))
    return part


def shards(features, weight, bias_vector, tile_nbrs, nbr_local, edge_count, cotangent):
    devices = lax.axis_size("coarse") * lax.axis_size("fine")
    position = lax.axis_index(GROUP)
    tile_count = features.shape[0] // TILE
    capacity = max(1, (NB - 1) * tile_count // (2 * (devices - 1)))
    slots = devices * capacity
    x_tiles = features.reshape(tile_count, TILE, C)
    cot_tiles = cotangent.reshape(tile_count, TILE, C)

    table = lax.all_to_all(
        jnp.broadcast_to(tile_nbrs.reshape(1, -1), (devices, NB * tile_count)),
        GROUP,
        split_axis=0,
        concat_axis=0,
        tiled=True,
    )
    packed, wanted = pack(position.reshape(1).astype(jnp.int32), table, x_tiles, capacity)
    arrived = exchange(packed, devices)

    nbr_local, edge_count, tile_nbrs, packed = lax.optimization_barrier(
        (nbr_local, edge_count, tile_nbrs, packed)
    )
    rows, columns = build_blocks(nbr_local, edge_count)
    owners = tile_nbrs // tile_count
    within = tile_nbrs % tile_count
    remote = owners != position
    onehot = (
        (owners.reshape(-1)[:, None] == jnp.arange(devices, dtype=jnp.int32)[None, :])
        & remote.reshape(-1)[:, None]
    ).astype(jnp.int32)
    ranking = jnp.sum((jnp.cumsum(onehot, axis=0) - onehot) * onehot, axis=1).reshape(owners.shape)
    buffer_slot = jnp.where(remote, owners * capacity + ranking, slots)
    rows_index = jnp.where(remote, tile_count + buffer_slot, within)
    held = (buffer_slot.reshape(-1)[None, :] == jnp.arange(slots, dtype=jnp.int32)[:, None]).astype(jnp.int32)
    source = jnp.sum(held * jnp.arange(NB * tile_count, dtype=jnp.int32)[None, :], axis=1)
    term_tile = source % tile_count
    term_slot = source // tile_count

    out, aggregated, preact_grad, gradient, terms = middle(
        rows_index, term_tile, term_slot, rows, columns, x_tiles, arrived, weight,
        bias_vector.reshape(1, C), cot_tiles, devices,
    )
    returned = exchange(terms, devices)
    aggregated, preact_grad, gradient, terms = lax.optimization_barrier(
        (aggregated, preact_grad, gradient, terms)
    )
    preact_grad = preact_grad.reshape(-1, C)
    weight_part = lax.dot_general(
        aggregated.reshape(-1, C), preact_grad, (((0,), (0,)), ((), ())), preferred_element_type=jnp.float32
    )
    bias_part = jnp.sum(preact_grad.astype(jnp.float32), axis=0)
    part = jnp.concatenate([weight_part, jnp.broadcast_to(bias_part[None], (C // 2, C))])
    summed = group_sum(part, devices, position)
    normalizer = 1.0 / math.sqrt(features.shape[0] * devices)
    summed = summed * normalizer
    local = local_terms(rows_index, columns, gradient)
    grad_features = final_sum(wanted, local, returned, devices)
    return (out.reshape(-1, C), grad_features.reshape(-1, C), summed[:C], summed[C])


def solution(mesh):
    return jax.shard_map(
        shards,
        mesh=mesh,
        in_specs=(
            P(("slab", "coarse", "fine"), None),
            P(),
            P(),
            P(None, ("slab", "coarse", "fine")),
            P(None, ("slab", "coarse", "fine")),
            P(None, ("slab", "coarse", "fine")),
            P(("slab", "coarse", "fine"), None),
        ),
        out_specs=(
            P(("slab", "coarse", "fine"), None),
            P(("slab", "coarse", "fine"), None),
            P("slab", None),
            P("slab"),
        ),
        check_vma=False,
    )
```

time: 439 us -> 318 us (0.72)
  other arithmetic: 137 us -> 5.62 us
  blocking collectives: 108 us -> 0 us
  Pallas kernels: 0 us -> 102 us
  waiting for transfers between devices: 75.8 us -> 144 us
  matrix products: 32.1 us -> 1 us
  local copies, waits for them, and re-layouts: 46.2 us -> 22.2 us
  starting transfers between devices: 24.6 us -> 40.5 us
  between operations: 14.2 us -> 0.93 us
    pallas_call x0 -> x5, Pallas kernels: none -> 102 us  [the longest x1 41.3 us: middle(): pl.pallas_call(middle_kernel, name='middle', in_specs=[whole(SMEM)] * 3 +...]
    psum x1 -> x0, blocking collectives: 94.5 us -> none  [shards(): lax.psum((weight_part, bias_part), ('coarse', 'fine'))]
    ppermute x0 -> x8, waiting for transfers between devices: none -> 93.7 us  [the longest x4 81.8 us: group_sum(): part = kept + lax.ppermute(sent, GROUP, pairs)]
    scatter-add x2 -> x0, other arithmetic: 62.2 us -> none  [the longest x1 43.3 us: shards(): jnp.zeros((tile_count + slots, TILE, C), jnp.float32).at[table_rows[1:].T]]
    psum x1 -> x0, waiting for transfers between devices: 41.4 us -> none  [shards(): lax.psum((weight_part, bias_part), ('coarse', 'fine'))]
    reduce_sum x2, other arithmetic: 41.7 us -> 0.95 us  [the longest x1 0.84 us: shards(): bias_part = jnp.sum(preact_grad.astype(jnp.float32), axis=0)]
    dot_general x5 -> x1, matrix products: 32.1 us -> 1 us  [shards(): lax.dot_general(aggregated.reshape(-1, C), preact_grad, (((0,), (0,)), ((...]
    slice x3, local copies, waits for them, and re-layouts: 18.9 us -> 1.47 us  [the longest x1 0.72 us: shards(): summed[:C]]
  transfers between devices with their start and end apart: 3 -> 11, of which waited for: 2 -> 9; matrix products, arithmetic and copies ran while one was open for 13% -> 3% of each run, Pallas kernels for 0% -> 16%
where the time goes in v1:
time: 318 us; the launch traced here: 317 us
  waiting for transfers between devices  144 us (45%)
  Pallas kernels  102 us (32%)
  starting transfers between devices  40.5 us (13%)
  local copies, waits for them, and re-layouts  22.2 us (7%)
  other arithmetic  5.62 us (2%)
    ppermute x4, waiting for transfers between devices, group_sum(): part = kept + lax.ppermute(sent, GROUP, pairs)  81.8 us
    all_to_all x2, waiting for transfers between devices, exchange(): lax.all_to_all(parted, GROUP, split_axis=0, concat_axis=0, tiled=True)  44.2 us
    pallas_call x1, Pallas kernels, middle(): pl.pallas_call(middle_kernel, name='middle', in_specs=[whole(SMEM)] * 3 +...  41.3 us
    pallas_call x1, Pallas kernels, build_blocks(): pl.pallas_call(blocks_kernel, name='blocks', grid=(tile_count,), in_specs...  25.3 us
    pallas_call x1, Pallas kernels, local_terms(): pl.pallas_call(local_kernel, name='local_terms', in_specs=[whole(SMEM), w...  25 us
    all_to_all x2, starting transfers between devices, exchange(): lax.all_to_all(parted, GROUP, split_axis=0, concat_axis=0, tiled=True)  24.6 us
    unnamed x31, local copies, waits for them, and re-layouts  19.1 us
    ppermute x4, waiting for transfers between devices, group_sum(): other = lax.ppermute(part, GROUP, pairs)  12 us
  transfers between devices with their start and end apart: 11, of which 9 were waited for; matrix products, arithmetic and copies ran while one was open for 3% of the time, Pallas kernels for 16%

profile of v1, /device:TPU:0, one launch (start us, length us, event | category | flops | bytes accessed | tf_op | source)
XLA Modules:
  0.0 316.7 jit_solution(2180448509569900831)
XLA Ops:
  0.6 0.8 broadcast_in_dim.10
  1.4 0.6 broadcast_in_dim.11
  2.0 7.4 %all-to-all-start = ((s32[16,1,192]{2,1,0:T(1,128)}), s32[16,1,192]{2,1,0:T(1,128)S(1)}, u32[]{:S(2)}, u32[]{:S(2)}) async-start(s32[16,1,192]{2,1,0:T(1,128)} %broadcast_in_dim.11), calls=%async_computation | async-start | bytes 32768 | tf_op jit(solution)/shard_map/all_to_all | solution.py:307
  9.4 6.5 %all-to-all-done = s32[16,1,192]{2,1,0:T(1,128)S(1)} async-done(((s32[16,1,192]{2,1,0:T(1,128)}), s32[16,1,192]{2,1,0:T(1,128)S(1)}, u32[]{:S(2)}, u32[]{:S(2)}) %all-to-all-start) | async-done | bytes 12320 | tf_op jit(solution)/shard_map/all_to_all | solution.py:307
  15.9 1.9 copy-done.4
  17.8 4.6 %pack.1 = (bf16[64,128,256]{2,1,0:T(8,128)(2,1)S(1)}, s32[16,128]{1,0:T(8,128)S(1)}) custom-call(s32[1]{0:T(128)} %bitcast.position_ref, s32[16,192]{1,0:T(8,128)S(1)} %bitcast.33, bf16[48,128,256]{2,1,0:T(8,128)(2,1)S(1)} %bitcast.31), custom_call_target="tpu_custom_call" | custom-call | tf_op jit(solution)/shard_map/pack/pallas_call | solution.py:66
  22.4 0.0 copy-start.6
  22.4 1.9 copy-done.6
  24.4 4.7 %all-to-all-start.1 = ((bf16[16,4,128,256]{3,2,1,0:T(8,128)(2,1)}), bf16[16,4,128,256]{3,2,1,0:T(8,128)(2,1)}, u32[]{:S(2)}, u32[]{:S(2)}) async-start(bf16[16,4,128,256]{3,2,1,0:T(8,128)(2,1)} %bitcast.32), calls=%async_computation.1 | async-start | bytes 8388608 | tf_op jit(solution)/shard_map/all_to_all | solution.py:278
  29.0 0.0 copy-done.13
  29.1 0.1 eq.57
  29.1 0.1 and.50
  29.3 0.6 reduce-window.6
  29.8 0.2 slice_reduce_fusion
  30.1 0.1 bitcast_bitcast_fusion
  30.2 0.1 reshape.71
  30.3 0.6 fusion.5
  30.9 0.1 eq.64
  30.9 0.0 copy-done.8
  30.9 0.0 copy-done.9
  30.9 25.3 %blocks.1 = (bf16[48,128,512]{2,1,0:T(8,128)(2,1)S(1)}, bf16[48,4,128,128]{3,2,1,0:T(8,128)(2,1)S(1)}) custom-call(s32[16,6144]{1,0:T(8,128)S(1)} %copy-done.8, s32[16,6144]{1,0:T(8,128)S(1)} %copy-done.9), custom_call_target="tpu_custom_call" | custom-call | tf_op jit(solution)/shard_map/blocks/pallas_call | solution.py:100
  56.3 0.0 copy-start.2
  56.3 2.7 copy-done.2
  59.0 2.6 copy-done.5
  61.6 0.1 select_reduce_fusion
  61.7 0.6 and_select_fusion
  62.3 44.2 %all-to-all-done.1 = bf16[16,4,128,256]{3,2,1,0:T(8,128)(2,1)} async-done(((bf16[16,4,128,256]{3,2,1,0:T(8,128)(2,1)}), bf16[16,4,128,256]{3,2,1,0:T(8,128)(2,1)}, u32[]{:S(2)}, u32[]{:S(2)}) %all-to-all-start.1) | async-done | bytes 4194336 | tf_op jit(solution)/shard_map/all_to_all | solution.py:278
  106.5 41.3 %middle.1 = (bf16[48,128,256]{2,1,0:T(8,128)(2,1)}, bf16[48,128,256]{2,1,0:T(8,128)(2,1)}, bf16[48,128,256]{2,1,0:T(8,128)(2,1)}, bf16[48,128,256]{2,1,0:T(8,128)(2,1)}, bf16[64,128,256]{2,1,0:T(8,128)(2,1)}) custom-call(s32[4,48]{1,0:T(4,128)} %get-tuple-element.34.rows_index.target_ref, s32[64]{0:T(128)} %get-tuple-element.39.term_tile, ...), custom_call_target="tpu_custom_call" | custom-call | tf_op jit(solution)/shard_map/middle/pallas_call | solution.py:180
  147.9 0.0 copy-start.11
  147.9 19.9 %all-to-all-start.2 = ((bf16[16,4,128,256]{3,2,1,0:T(8,128)(2,1)}), bf16[16,4,128,256]{3,2,1,0:T(8,128)(2,1)}, u32[]{:S(2)}, u32[]{:S(2)}) async-start(bf16[16,4,128,256]{3,2,1,0:T(8,128)(2,1)} %bitcast.34), calls=%async_computation.2 | async-start | bytes 8388608 | tf_op jit(solution)/shard_map/all_to_all | solution.py:278
  167.8 0.0 copy-start.14
  167.8 0.0 copy-done.11
  167.8 0.8 convert_reduce_fusion
  168.7 1.0 copy-done.14
  169.7 1.0 convolution_bitcast_fusion
  170.7 0.0 copy-start.7
  170.8 0.7 slice_select_fusion
  171.5 0.4 collective-permute-start
  171.8 1.4 collective-permute-done
  173.2 1.0 select_add_fusion
  174.2 0.7 copy-done.12
  174.9 1.9 collective-permute-start.1
  176.9 19.6 %collective-permute-done.1 = f32[96,256]{1,0:T(8,128)S(1)} collective-permute-done((f32[96,256]{1,0:T(8,128)S(1)}, f32[96,256]{1,0:T(8,128)S(1)}, u32[]{:S(2)}, u32[]{:S(2)}) %collective-permute-start.1) | collective-permute-done | bytes 98336 | tf_op jit(solution)/shard_map/ppermute | solution.py:289
  196.4 1.0 select_add_fusion.1
  197.4 0.1 collective-permute-start.2
  197.5 40.0 %collective-permute-done.2 = f32[48,256]{1,0:T(8,128)S(1)} collective-permute-done((f32[48,256]{1,0:T(8,128)S(1)}, f32[48,256]{1,0:T(8,128)S(1)}, u32[]{:S(2)}, u32[]{:S(2)}) %collective-permute-start.2) | collective-permute-done | bytes 49184 | tf_op jit(solution)/shard_map/ppermute | solution.py:289
  237.5 4.5 %collective-permute-start.3 = (f32[24,256]{1,0:T(8,128)S(1)}, f32[24,256]{1,0:T(8,128)S(1)}, u32[]{:S(2)}, u32[]{:S(2)}) collective-permute-start(f32[24,256]{1,0:T(8,128)S(1)} %slice_select_fusion.3), channel_id=1, source_target_pairs={{0,8},{1,9},{2,10},{3,11},{4,12},{5,13},{6,14},{7,15},{8,0},{9,1},... | collective-permute-start | bytes 73736 | tf_op jit(solution)/shard_map/ppermute | solution.py:289
  242.0 20.8 %collective-permute-done.3 = f32[24,256]{1,0:T(8,128)S(1)} collective-permute-done((f32[24,256]{1,0:T(8,128)S(1)}, f32[24,256]{1,0:T(8,128)S(1)}, u32[]{:S(2)}, u32[]{:S(2)}) %collective-permute-start.3) | collective-permute-done | bytes 24608 | tf_op jit(solution)/shard_map/ppermute | solution.py:289
  262.8 0.0 collective-permute-start.4
  262.9 4.7 %collective-permute-done.4 = f32[24,256]{1,0:T(8,128)S(1)} collective-permute-done((f32[24,256]{1,0:T(8,128)S(1)}, f32[24,256]{1,0:T(8,128)S(1)}, u32[]{:S(2)}, u32[]{:S(2)}) %collective-permute-start.4) | collective-permute-done | bytes 24608 | tf_op jit(solution)/shard_map/ppermute | solution.py:293
  267.6 0.0 collective-permute-start.5
  267.6 4.1 %collective-permute-done.5 = f32[48,256]{1,0:T(8,128)S(1)} collective-permute-done((f32[48,256]{1,0:T(8,128)S(1)}, f32[48,256]{1,0:T(8,128)S(1)}, u32[]{:S(2)}, u32[]{:S(2)}) %collective-permute-start.5) | collective-permute-done | bytes 49184 | tf_op jit(solution)/shard_map/ppermute | solution.py:293
  271.7 1.5 collective-permute-start.6
  273.2 3.2 collective-permute-done.6
  276.4 0.1 collective-permute-start.7
  276.5 2.8 copy-done.3
  279.3 25.0 %local_terms.1.local_ref = f32[48,128,256]{2,1,0:T(8,128)S(1)} custom-call(s32[4,48]{1,0:T(4,128)S(1)} %copy-done.10, bf16[48,4,128,128]{3,2,1,0:T(8,128)(2,1)S(1)} %copy-done.3, bf16[48,128,256]{2,1,0:T(8,128)(2,1)S(1)} %copy-done.7), custom_call_target="tpu_custom_call" | custom-call | tf_op jit(solution)/shard_map/local_terms/pallas_call | solution.py:221
  304.3 2.7 copy-done
  307.0 0.0 collective-permute-done.7
  307.0 0.7 slice.69
  307.7 0.6 slice.70
  308.3 0.0 all-to-all-done.2
  308.3 2.8 copy-done.1
  311.1 5.6 %final_sum.1 = bf16[48,128,256]{2,1,0:T(8,128)(2,1)} custom-call(s32[16,128]{1,0:T(8,128)S(1)} %get-tuple-element.26.wanted_ref, f32[48,128,256]{2,1,0:T(8,128)S(1)} %copy-done.1, bf16[64,128,256]{2,1,0:T(8,128)(2,1)} %bitcast.9.returned_ref), custom_call_target="tpu_custom_call" | custom-call | tf_op jit(solution)/shard_map/final_sum/pallas_call | solution.py:260
  (29 shorter events, 0.3 us)
Async XLA Ops:
  2.0 13.9 %all-to-all-start = ((s32[16,1,192]{2,1,0:T(1,128)}), s32[16,1,192]{2,1,0:T(1,128)S(1)}, u32[]{:S(2)}, u32[]{:S(2)}) async-start(s32[16,1,192]{2,1,0:T(1,128)} %broadcast_in_dim.11), calls=%async_computation | async-start | bytes 32768 | tf_op jit(solution)/shard_map/all_to_all | solution.py:307
  15.9 1.9 copy-start.4
  22.4 1.9 copy-start.6
  24.4 4.7 %copy-start.13 = (s32[4,48]{1,0:T(4,128)S(1)}, s32[4,48]{1,0:T(4,128)}, u32[]{:S(2)}) copy-start(s32[4,48]{1,0:T(4,128)} %param.10) | copy-start | bytes 2308
  24.4 6.6 %copy-start.8 = (s32[16,6144]{1,0:T(8,128)S(1)}, s32[16,6144]{1,0:T(8,128)}, u32[]{:S(2)}) copy-start(s32[16,6144]{1,0:T(8,128)} %nbr_ref) | copy-start | bytes 1179652
  24.4 6.6 %copy-start.9 = (s32[16,6144]{1,0:T(8,128)S(1)}, s32[16,6144]{1,0:T(8,128)}, u32[]{:S(2)}) copy-start(s32[16,6144]{1,0:T(8,128)} %count_ref) | copy-start | bytes 1179652
  24.4 82.1 %all-to-all-start.1 = ((bf16[16,4,128,256]{3,2,1,0:T(8,128)(2,1)}), bf16[16,4,128,256]{3,2,1,0:T(8,128)(2,1)}, u32[]{:S(2)}, u32[]{:S(2)}) async-start(bf16[16,4,128,256]{3,2,1,0:T(8,128)(2,1)} %bitcast.32), calls=%async_computation.1 | async-start | bytes 8388608 | tf_op jit(solution)/shard_map/all_to_all | solution.py:278
  56.3 2.7 copy-start.2
  59.0 2.6 copy-start.5
  147.9 20.0 %copy-start.11 = (bf16[48,128,256]{2,1,0:T(8,128)(2,1)S(1)}, bf16[48,128,256]{2,1,0:T(8,128)(2,1)}, u32[]{:S(2)}) copy-start(bf16[48,128,256]{2,1,0:T(8,128)(2,1)} %get-tuple-element.33) | copy-start | bytes 9437188
  147.9 160.4 %all-to-all-start.2 = ((bf16[16,4,128,256]{3,2,1,0:T(8,128)(2,1)}), bf16[16,4,128,256]{3,2,1,0:T(8,128)(2,1)}, u32[]{:S(2)}, u32[]{:S(2)}) async-start(bf16[16,4,128,256]{3,2,1,0:T(8,128)(2,1)} %bitcast.34), calls=%async_computation.2 | async-start | bytes 8388608 | tf_op jit(solution)/shard_map/all_to_all | solution.py:278
  167.8 1.9 copy-start.14
  170.7 105.7 %copy-start.7 = (bf16[48,128,256]{2,1,0:T(8,128)(2,1)S(1)}, bf16[48,128,256]{2,1,0:T(8,128)(2,1)}, u32[]{:S(2)}) copy-start(bf16[48,128,256]{2,1,0:T(8,128)(2,1)} %get-tuple-element.31.grad_ref) | copy-start | bytes 9437188
  170.7 105.7 %copy-start.10 = (s32[4,48]{1,0:T(4,128)S(1)}, s32[4,48]{1,0:T(4,128)}, u32[]{:S(2)}) copy-start(s32[4,48]{1,0:T(4,128)} %get-tuple-element.34.rows_index.target_ref) | copy-start | bytes 2308
  171.5 1.8 collective-permute-start
  174.2 0.7 copy-start.12
  174.9 21.5 %collective-permute-start.1 = (f32[96,256]{1,0:T(8,128)S(1)}, f32[96,256]{1,0:T(8,128)S(1)}, u32[]{:S(2)}, u32[]{:S(2)}) collective-permute-start(f32[96,256]{1,0:T(8,128)S(1)} %slice_select_fusion.1), channel_id=1, source_target_pairs={{0,2},{1,3},{2,0},{3,1},{4,6},{5,7},{6,4},{7,5},{8,10},{9,11},{10,... | collective-permute-start | bytes 294920 | tf_op jit(solution)/shard_map/ppermute | solution.py:289
  197.4 40.0 %collective-permute-start.2 = (f32[48,256]{1,0:T(8,128)S(1)}, f32[48,256]{1,0:T(8,128)S(1)}, u32[]{:S(2)}, u32[]{:S(2)}) collective-permute-start(f32[48,256]{1,0:T(8,128)S(1)} %slice_select_fusion.2), channel_id=1, source_target_pairs={{0,4},{1,5},{2,6},{3,7},{4,0},{5,1},{6,2},{7,3},{8,12},{9,13},{10,... | collective-permute-start | bytes 147464 | tf_op jit(solution)/shard_map/ppermute | solution.py:289
  237.5 25.4 %collective-permute-start.3 = (f32[24,256]{1,0:T(8,128)S(1)}, f32[24,256]{1,0:T(8,128)S(1)}, u32[]{:S(2)}, u32[]{:S(2)}) collective-permute-start(f32[24,256]{1,0:T(8,128)S(1)} %slice_select_fusion.3), channel_id=1, source_target_pairs={{0,8},{1,9},{2,10},{3,11},{4,12},{5,13},{6,14},{7,15},{8,0},{9,1},... | collective-permute-start | bytes 73736 | tf_op jit(solution)/shard_map/ppermute | solution.py:289
  262.8 4.7 %collective-permute-start.4 = (f32[24,256]{1,0:T(8,128)S(1)}, f32[24,256]{1,0:T(8,128)S(1)}, u32[]{:S(2)}, u32[]{:S(2)}) collective-permute-start(f32[24,256]{1,0:T(8,128)S(1)} %select_add_fusion.3), channel_id=1, source_target_pairs={{0,8},{1,9},{2,10},{3,11},{4,12},{5,13},{6,14},{7,15},{8,0},{9,1},... | collective-permute-start | bytes 73736 | tf_op jit(solution)/shard_map/ppermute | solution.py:293
  267.6 4.1 %collective-permute-start.5 = (f32[48,256]{1,0:T(8,128)S(1)}, f32[48,256]{1,0:T(8,128)S(1)}, u32[]{:S(2)}, u32[]{:S(2)}) collective-permute-start(f32[48,256]{1,0:T(8,128)S(1)} %maximum_select_fusion.3), channel_id=1, source_target_pairs={{0,4},{1,5},{2,6},{3,7},{4,0},{5,1},{6,2},{7,3},{8,12},{9,13},{10,... | collective-permute-start | bytes 147464 | tf_op jit(solution)/shard_map/ppermute | solution.py:293
  271.7 4.7 %collective-permute-start.6 = (f32[96,256]{1,0:T(8,128)S(1)}, f32[96,256]{1,0:T(8,128)S(1)}, u32[]{:S(2)}, u32[]{:S(2)}) collective-permute-start(f32[96,256]{1,0:T(8,128)S(1)} %maximum_select_fusion.2), channel_id=1, source_target_pairs={{0,2},{1,3},{2,0},{3,1},{4,6},{5,7},{6,4},{7,5},{8,10},{9,11},{10,... | collective-permute-start | bytes 294920 | tf_op jit(solution)/shard_map/ppermute | solution.py:293
  276.4 30.6 %collective-permute-start.7 = (f32[192,256]{1,0:T(8,128)S(1)}, f32[192,256]{1,0:T(8,128)S(1)}, u32[]{:S(2)}, u32[]{:S(2)}) collective-permute-start(f32[192,256]{1,0:T(8,128)S(1)} %maximum_select_fusion.1), channel_id=1, source_target_pairs={{0,1},{1,0},{2,3},{3,2},{4,5},{5,4},{6,7},{7,6},{8,9},{9,8},{10,11... | collective-permute-start | bytes 589832 | tf_op jit(solution)/shard_map/ppermute | solution.py:293
  276.5 2.8 copy-start.3
  304.3 2.7 copy-start
  308.3 2.8 copy-start.1

commit v2 on v1

--- a/solution.py
+++ b/solution.py
@@ -13,16 +13,21 @@
 GROUP = ("coarse", "fine")
 VMEM = pltpu.MemorySpace.VMEM
 SMEM = pltpu.MemorySpace.SMEM
+HBM = pltpu.MemorySpace.HBM
+PIECE = 32
+MIDDLE_VMEM = 20 << 20
 
 
 def whole(space=VMEM):
     return pl.BlockSpec(memory_space=space)
 
 
-def pack_kernel(position_ref, table_ref, x_ref, packed_ref, wanted_ref, wanted_s, table_sem, sems):
+def pack_kernel(position_ref, table_ref, x_ref, packed_ref, wanted_ref, x_held, wanted_s, x_sem, table_sem, sems):
     devices, slot_count = table_ref.shape
     tile_count = x_ref.shape[0]
     capacity = packed_ref.shape[0] // devices
+    load = pltpu.make_async_copy(x_ref, x_held, x_sem)
+    load.start()
     position = position_ref[0]
     within = table_ref[...] - position * tile_count
     asker = lax.broadcasted_iota(jnp.int32, within.shape, 0)
@@ -42,23 +47,24 @@
     copy = pltpu.make_async_copy(wanted_ref, wanted_s, table_sem)
     copy.start()
     copy.wait()
-    for device in range(devices):
-        for rank in range(capacity):
-            tile = wanted_s[device, rank]
-
-            @pl.when(tile >= 0)
-            def _():
-                slot = device * capacity + rank
-                pltpu.make_async_copy(x_ref.at[tile], packed_ref.at[slot], sems.at[slot]).start()
-
-    for device in range(devices):
-        for rank in range(capacity):
-            tile = wanted_s[device, rank]
-
-            @pl.when(tile >= 0)
-            def _():
-                slot = device * capacity + rank
-                pltpu.make_async_copy(x_ref.at[tile], packed_ref.at[slot], sems.at[slot]).wait()
+    load.wait()
+
+    def each(act):
+        def step(device, carry):
+            for rank in range(capacity):
+                tile = wanted_s[device, rank]
+
+                @pl.when(tile >= 0)
+                def _():
+                    slot = device * capacity + rank
+                    act(pltpu.make_async_copy(x_held.at[tile], packed_ref.at[slot], sems.at[slot]))
+
+            return carry
+
+        lax.fori_loop(0, devices, step, 0)
+
+    each(lambda copy: copy.start())
+    each(lambda copy: copy.wait())
 
 
 def pack(position, table, x_tiles, capacity):
@@ -66,14 +72,16 @@
     return pl.pallas_call(
         pack_kernel,
         name="pack",
-        in_specs=[whole(SMEM), whole(), whole()],
-        out_specs=[pl.BlockSpec(memory_space=pl.ANY), whole()],
+        in_specs=[whole(SMEM), whole(), whole(HBM)],
+        out_specs=[whole(HBM), whole()],
         out_shape=[
             jax.ShapeDtypeStruct((devices * capacity, TILE, C), jnp.bfloat16),
             jax.ShapeDtypeStruct((devices, 128), jnp.int32),
         ],
         scratch_shapes=[
+            pltpu.VMEM(x_tiles.shape, jnp.bfloat16),
             pltpu.SMEM((devices, 128), jnp.int32),
+            pltpu.SemaphoreType.DMA,
             pltpu.SemaphoreType.DMA,
             pltpu.SemaphoreType.DMA((devices * capacity,)),
         ],
@@ -115,49 +123,57 @@
 
 
 def middle_kernel(
-    rows_index, term_tile, term_slot, rows_ref, columns_ref, x_ref, arrived_ref, weight_ref, bias_ref, cot_ref,
-    out_ref, agg_ref, pg_ref, grad_ref, terms_ref, near, terms, near_sems, sems,
+    rows_index, term_tile, rows_ref, sent_ref, x_ref, arrived_ref, weight_ref, bias_ref, cot_ref,
+    out_ref, agg_ref, pg_ref, grad_ref, terms_ref, near, terms, pre, near_sems, sems,
 ):
     tile_count = x_ref.shape[0]
     slots = arrived_ref.shape[0]
+    group = pre.shape[0] // TILE
+    others = pltpu.make_async_copy(arrived_ref, near.at[pl.ds(tile_count, slots)], near_sems.at[1])
+    others.start()
     own = pltpu.make_async_copy(x_ref, near.at[pl.ds(0, tile_count)], near_sems.at[0])
-    others = pltpu.make_async_copy(arrived_ref, near.at[pl.ds(tile_count, slots)], near_sems.at[1])
     own.start()
-    others.start()
     own.wait()
     others.wait()
     weight = weight_ref[...]
     bias = bias_ref[...]
 
-    def tile_step(t, carry):
-        rows = rows_ref[t]
-        first = jnp.concatenate([near[t], near[rows_index[1, t]]], axis=0)
-        second = jnp.concatenate([near[rows_index[2, t]], near[rows_index[3, t]]], axis=0)
-        total = jnp.dot(rows[:, : 2 * TILE], first, preferred_element_type=jnp.float32)
-        total += jnp.dot(rows[:, 2 * TILE :], second, preferred_element_type=jnp.float32)
-        aggregated = total.astype(jnp.bfloat16)
-        agg_ref[t] = aggregated
-        preact = jnp.dot(aggregated, weight, preferred_element_type=jnp.float32) + bias
-        sigma = jax.nn.sigmoid(preact)
-        out_ref[t] = (preact * sigma).astype(jnp.bfloat16)
-        slope = sigma * (1.0 + preact * (1.0 - sigma))
-        preact_grad = (cot_ref[t].astype(jnp.float32) * slope).astype(jnp.bfloat16)
-        pg_ref[t] = preact_grad
-        grad_ref[t] = lax.dot_general(
+    def group_step(step, carry):
+        start = step * group
+        for at in range(group):
+            t = start + at
+            rows = rows_ref[t]
+            first = jnp.concatenate([near[t], near[rows_index[1, t]]], axis=0)
+            second = jnp.concatenate([near[rows_index[2, t]], near[rows_index[3, t]]], axis=0)
+            total = jnp.dot(rows[:, : 2 * TILE], first, preferred_element_type=jnp.float32)
+            total += jnp.dot(rows[:, 2 * TILE :], second, preferred_element_type=jnp.float32)
+            agg_ref[t] = total.astype(jnp.bfloat16)
+        aggregated = agg_ref[pl.ds(start, group)].reshape(group * TILE, C)
+        pre[...] = jnp.dot(aggregated, weight, preferred_element_type=jnp.float32) + bias
+        for piece in range(group * TILE // PIECE):
+            t = start + piece * PIECE // TILE
+            part = pl.ds(piece * PIECE % TILE, PIECE)
+            preact = pre[piece * PIECE : (piece + 1) * PIECE]
+            sigma = jax.nn.sigmoid(preact)
+            out_ref[t, part] = (preact * sigma).astype(jnp.bfloat16)
+            slope = sigma * (1.0 + preact * (1.0 - sigma))
+            pg_ref[t, part] = (cot_ref[t, part].astype(jnp.float32) * slope).astype(jnp.bfloat16)
+        preact_grad = pg_ref[pl.ds(start, group)].reshape(group * TILE, C)
+        gradient = lax.dot_general(
             preact_grad, weight, (((1,), (1,)), ((), ())), preferred_element_type=jnp.float32
-        ).astype(jnp.bfloat16)
-        return carry
-
-    lax.fori_loop(0, tile_count, tile_step, 0)
+        )
+        grad_ref[pl.ds(start, group)] = gradient.astype(jnp.bfloat16).reshape(group, TILE, C)
+        return carry
+
+    lax.fori_loop(0, tile_count // group, group_step, 0)
 
     per = slots // sems.shape[0]
 
     def term_step(device, carry):
         for rank in range(per):
             slot = device * per + rank
-            t = term_tile[slot]
             terms[slot] = jnp.dot(
-                columns_ref[t, term_slot[slot]], grad_ref[t], preferred_element_type=jnp.float32
+                sent_ref[slot], grad_ref[term_tile[slot]], preferred_element_type=jnp.float32
             ).astype(jnp.bfloat16)
         part = pl.ds(device * per, per)
         pltpu.make_async_copy(terms.at[part], terms_ref.at[part], sems.at[device]).start()
@@ -173,24 +189,26 @@
     lax.fori_loop(0, sems.shape[0], finish, 0)
 
 
-def middle(rows_index, term_tile, term_slot, rows, columns, x_tiles, arrived, weight, bias, cot, devices):
+def middle(rows_index, term_tile, rows, sent, x_tiles, arrived, weight, bias, cot, devices):
     tile_count = x_tiles.shape[0]
     slots = arrived.shape[0]
+    group = math.gcd(tile_count, 8)
     tiles = jax.ShapeDtypeStruct((tile_count, TILE, C), jnp.bfloat16)
     return pl.pallas_call(
         middle_kernel,
         name="middle",
-        in_specs=[whole(SMEM)] * 3 + [whole()] * 3 + [pl.BlockSpec(memory_space=pl.ANY)] + [whole()] * 3,
-        out_specs=[whole()] * 4 + [pl.BlockSpec(memory_space=pl.ANY)],
+        in_specs=[whole(SMEM)] * 2 + [whole()] * 3 + [whole(HBM)] + [whole()] * 3,
+        out_specs=[whole()] * 4 + [whole(HBM)],
         out_shape=[tiles] * 4 + [jax.ShapeDtypeStruct((slots, TILE, C), jnp.bfloat16)],
         scratch_shapes=[
             pltpu.VMEM((tile_count + slots, TILE, C), jnp.bfloat16),
             pltpu.VMEM((slots, TILE, C), jnp.bfloat16),
+            pltpu.VMEM((group * TILE, C), jnp.float32),
             pltpu.SemaphoreType.DMA((2,)),
             pltpu.SemaphoreType.DMA((devices,)),
         ],
-        compiler_params=pltpu.CompilerParams(vmem_limit_bytes=58 << 20),
-    )(rows_index, term_tile, term_slot, rows, columns, x_tiles, arrived, weight, bias, cot)
+        compiler_params=pltpu.CompilerParams(vmem_limit_bytes=MIDDLE_VMEM),
+    )(rows_index, term_tile, rows, sent, x_tiles, arrived, weight, bias, cot)
 
 
 def local_kernel(target_ref, columns_ref, grad_ref, total_ref):
@@ -278,19 +296,30 @@
     return lax.all_to_all(parted, GROUP, split_axis=0, concat_axis=0, tiled=True).reshape(array.shape)
 
 
-def group_sum(part, devices, position):
+def group_sum(part, devices, position, hold):
     bits = devices.bit_length() - 1
-    for bit in range(bits):
+    low = bits - 2
+
+    def swap(piece, difference):
+        return lax.ppermute(piece, GROUP, [(d, d ^ difference) for d in range(devices)])
+
+    for bit in range(low):
         half = part.shape[0] // 2
         upper = (position >> bit) & 1 == 1
-        pairs = [(d, d ^ (1 << bit)) for d in range(devices)]
-        sent = jnp.where(upper, part[:half], part[half:])
+        got = swap(jnp.where(upper, part[:half], part[half:]), 1 << bit)
         kept = jnp.where(upper, part[half:], part[:half])
-        part = kept + lax.ppermute(sent, GROUP, pairs)
-    for bit in reversed(range(bits)):
+        if bit == low - 1:
+            got = hold(got)
+        part = kept + got
+    quarters = part.reshape(4, part.shape[0] // 4, C)
+    place = position >> low
+    got = [swap(lax.dynamic_index_in_dim(quarters, place ^ r, 0, False), r << low) for r in range(1, 4)]
+    part = lax.dynamic_index_in_dim(quarters, place, 0, False) + got[0] + got[1] + got[2]
+    gathered = jnp.stack([part] + [swap(part, r << low) for r in range(1, 4)])
+    part = jnp.concatenate([lax.dynamic_index_in_dim(gathered, place ^ j, 0, False) for j in range(4)])
+    for bit in reversed(range(low)):
         upper = (position >> bit) & 1 == 1
-        pairs = [(d, d ^ (1 << bit)) for d in range(devices)]
-        other = lax.ppermute(part, GROUP, pairs)
+        other = swap(part, 1 << bit)
         part = jnp.where(upper, jnp.concatenate([other, part]), jnp.concatenate([part, other]))
     return part
 
@@ -332,9 +361,10 @@
     source = jnp.sum(held * jnp.arange(NB * tile_count, dtype=jnp.int32)[None, :], axis=1)
     term_tile = source % tile_count
     term_slot = source // tile_count
+    sent = columns.reshape(NB * tile_count, TILE, TILE)[term_tile * NB + term_slot]
 
     out, aggregated, preact_grad, gradient, terms = middle(
-        rows_index, term_tile, term_slot, rows, columns, x_tiles, arrived, weight,
+        rows_index, term_tile, rows, sent, x_tiles, arrived, weight,
         bias_vector.reshape(1, C), cot_tiles, devices,
     )
     returned = exchange(terms, devices)
@@ -347,10 +377,10 @@
     )
     bias_part = jnp.sum(preact_grad.astype(jnp.float32), axis=0)
     part = jnp.concatenate([weight_part, jnp.broadcast_to(bias_part[None], (C // 2, C))])
-    summed = group_sum(part, devices, position)
+    local = local_terms(rows_index, columns, gradient)
+    summed = group_sum(part, devices, position, lambda got: lax.optimization_barrier((got, local))[0])
     normalizer = 1.0 / math.sqrt(features.shape[0] * devices)
     summed = summed * normalizer
-    local = local_terms(rows_index, columns, gradient)
     grad_features = final_sum(wanted, local, returned, devices)
     return (out.reshape(-1, C), grad_features.reshape(-1, C), summed[:C], summed[C])
 

time: 318 us -> 276 us (0.87)
  waiting for transfers between devices: 144 us -> 92.5 us
  local copies, waits for them, and re-layouts: 22.2 us -> 49.3 us
  Pallas kernels: 102 us -> 75.2 us
  starting transfers between devices: 40.5 us -> 45.1 us
  other arithmetic: 5.62 us -> 10.2 us
    ppermute x8 -> x10, waiting for transfers between devices: 93.7 us -> 61.4 us  [swap(): lax.ppermute(piece, GROUP, [(d, d ^ difference) for d in range(devices)])]
    pallas_call x1, Pallas kernels: 41.3 us -> 14.6 us  [middle(): pl.pallas_call(middle_kernel, name='middle', in_specs=[whole(SMEM)] * 2 +...]
    all_to_all x2, waiting for transfers between devices: 44.2 us -> 24.6 us  [exchange(): lax.all_to_all(parted, GROUP, split_axis=0, concat_axis=0, tiled=True)]
    unnamed x31 -> x54, local copies, waits for them, and re-layouts: 19.1 us -> 34.5 us
    gather x0 -> x1, local copies, waits for them, and re-layouts: none -> 4.92 us  [shards(): columns.reshape(NB * tile_count, TILE, TILE)[term_tile * NB + term_slot]]
    ppermute x8 -> x10, starting transfers between devices: 8.5 us -> 13.1 us  [swap(): lax.ppermute(piece, GROUP, [(d, d ^ difference) for d in range(devices)])]
    another operation x4 -> x5, other arithmetic: 0.71 us -> 4.54 us
  transfers between devices with their start and end apart: 11 -> 13, of which waited for: 9 -> 9; matrix products, arithmetic and copies ran while one was open for 3% -> 9% of each run, Pallas kernels for 16% -> 18%
where the time goes in v2:
time: 276 us; the launch traced here: 274 us
  waiting for transfers between devices  92.5 us (34%)
  Pallas kernels  75.2 us (27%)
  local copies, waits for them, and re-layouts  49.3 us (18%)
  starting transfers between devices  45.1 us (16%)
  other arithmetic  10.2 us (4%)
    ppermute x10, waiting for transfers between devices, swap(): lax.ppermute(piece, GROUP, [(d, d ^ difference) for d in range(devices)])  61.4 us
    unnamed x54, local copies, waits for them, and re-layouts  34.5 us
    pallas_call x1, Pallas kernels, build_blocks(): pl.pallas_call(blocks_kernel, name='blocks', grid=(tile_count,), in_specs...  25.3 us
    pallas_call x1, Pallas kernels, local_terms(): pl.pallas_call(local_kernel, name='local_terms', in_specs=[whole(SMEM), w...  24.8 us
    all_to_all x2, starting transfers between devices, exchange(): lax.all_to_all(parted, GROUP, split_axis=0, concat_axis=0, tiled=True)  24.6 us
    all_to_all x2, waiting for transfers between devices, exchange(): lax.all_to_all(parted, GROUP, split_axis=0, concat_axis=0, tiled=True)  24.6 us
    pallas_call x1, Pallas kernels, middle(): pl.pallas_call(middle_kernel, name='middle', in_specs=[whole(SMEM)] * 2 +...  14.6 us
    ppermute x10, starting transfers between devices, swap(): lax.ppermute(piece, GROUP, [(d, d ^ difference) for d in range(devices)])  13.1 us
  transfers between devices with their start and end apart: 13, of which 9 were waited for; matrix products, arithmetic and copies ran while one was open for 9% of the time, Pallas kernels for 18%

profile of v2, /device:TPU:0, one launch (start us, length us, event | category | flops | bytes accessed | tf_op | source)
XLA Modules:
  0.0 274.4 jit_solution(9818857568207581197)
XLA Ops:
  0.6 0.8 broadcast_in_dim.10
  1.4 0.6 broadcast_in_dim.11
  2.0 7.4 %all-to-all-start = ((s32[16,1,192]{2,1,0:T(1,128)}), s32[16,1,192]{2,1,0:T(1,128)S(1)}, u32[]{:S(2)}, u32[]{:S(2)}) async-start(s32[16,1,192]{2,1,0:T(1,128)} %broadcast_in_dim.11), calls=%async_computation | async-start | bytes 32768 | tf_op jit(solution)/shard_map/all_to_all | solution.py:336
  9.4 6.5 %all-to-all-done = s32[16,1,192]{2,1,0:T(1,128)S(1)} async-done(((s32[16,1,192]{2,1,0:T(1,128)}), s32[16,1,192]{2,1,0:T(1,128)S(1)}, u32[]{:S(2)}, u32[]{:S(2)}) %all-to-all-start) | async-done | bytes 12320 | tf_op jit(solution)/shard_map/all_to_all | solution.py:336
  15.9 1.9 copy-done.2
  17.8 4.9 %pack.1 = (bf16[64,128,256]{2,1,0:T(8,128)(2,1)S(1)}, s32[16,128]{1,0:T(8,128)S(1)}) custom-call(s32[1]{0:T(128)} %bitcast.position_ref, s32[16,192]{1,0:T(8,128)S(1)} %bitcast.86, bf16[48,128,256]{2,1,0:T(8,128)(2,1)S(1)} %bitcast.80), custom_call_target="tpu_custom_call" | custom-call | tf_op jit(solution)/shard_map/pack/pallas_call | solution.py:72
  22.8 2.0 copy-done.10
  24.7 4.7 %all-to-all-start.1 = ((bf16[16,4,128,256]{3,2,1,0:T(8,128)(2,1)}), bf16[16,4,128,256]{3,2,1,0:T(8,128)(2,1)}, u32[]{:S(2)}, u32[]{:S(2)}) async-start(bf16[16,4,128,256]{3,2,1,0:T(8,128)(2,1)} %bitcast.84), calls=%async_computation.1 | async-start | bytes 8388608 | tf_op jit(solution)/shard_map/all_to_all | solution.py:296
  29.4 0.6 broadcast_compare_fusion
  30.0 1.1 eq.49
  31.1 1.3 and.58
  32.4 0.7 fusion.6
  33.0 0.6 copy_bitcast_fusion
  33.6 1.9 reduce-window.6
  35.5 1.5 slice_reduce_fusion
  37.0 1.3 reduce-window.9
  38.3 0.7 slice.32
  38.9 0.8 bitcast_bitcast_fusion
  39.7 1.3 fusion.4
  41.0 1.3 reshape.139
  42.3 1.3 fusion.7
  43.6 1.3 eq.56
  44.9 1.0 copy-done.17
  45.9 25.3 %blocks.1 = (bf16[48,128,512]{2,1,0:T(8,128)(2,1)S(1)}, bf16[48,4,128,128]{3,2,1,0:T(8,128)(2,1)S(1)}) custom-call(s32[16,6144]{1,0:T(8,128)S(1)} %copy-done.16, s32[16,6144]{1,0:T(8,128)S(1)} %copy-done.17), custom_call_target="tpu_custom_call" | custom-call | tf_op jit(solution)/shard_map/blocks/pallas_call | solution.py:108
  71.3 2.6 copy-done.4
  73.9 2.6 copy-done.7
  76.5 0.8 select_reduce_fusion
  77.4 4.9 %gather_fusion = bf16[64,128,128]{2,1,0:T(8,128)(2,1)} fusion(bf16[192,128,128]{2,1,0:T(8,128)(2,1)} %bitcast.82, s32[1024]{0:T(1024)S(1)} %pad_clamp_fusion), kind=kCustom, calls=%fused_computation | custom fusion | bytes 4194560 | tf_op jit(solution)/shard_map/gather | solution.py:364
  82.3 24.6 %all-to-all-done.1 = bf16[16,4,128,256]{3,2,1,0:T(8,128)(2,1)} async-done(((bf16[16,4,128,256]{3,2,1,0:T(8,128)(2,1)}), bf16[16,4,128,256]{3,2,1,0:T(8,128)(2,1)}, u32[]{:S(2)}, u32[]{:S(2)}) %all-to-all-start.1) | async-done | bytes 4194336 | tf_op jit(solution)/shard_map/all_to_all | solution.py:296
  106.9 1.6 copy-done.6
  108.5 2.8 %copy-done.8 = bf16[48,128,512]{2,1,0:T(8,128)(2,1)S(1)} copy-done((bf16[48,128,512]{2,1,0:T(8,128)(2,1)S(1)}, bf16[48,128,512]{2,1,0:T(8,128)(2,1)}, u32[]{:S(2)}) %copy-start.8) | copy-done | bytes 6291480
  111.3 1.9 copy-done.15
  113.2 14.6 %middle.1 = (bf16[48,128,256]{2,1,0:T(8,128)(2,1)}, bf16[48,128,256]{2,1,0:T(8,128)(2,1)S(1)}, bf16[48,128,256]{2,1,0:T(8,128)(2,1)S(1)}, bf16[48,128,256]{2,1,0:T(8,128)(2,1)S(1)}, bf16[64,128,256]{2,1,0:T(8,128)(2,1)S(1)}) custom-call(s32[4,48]{1,0:T(4,128)S(1)} %get-tuple-element.44.rows_index.target_ref, s32[64]{0:T(128)S(1)} %and_select_fusion.1.term_tile, ...), custom_call_target="tpu_custom_call" | custom-call | tf_op jit(solution)/shard_map/middle/pallas_call | solution.py:197
  127.8 2.0 copy-done.9
  129.9 1.6 copy-done.11
  131.5 1.7 copy-done.13
  133.2 1.6 copy-done.20
  134.8 19.9 %all-to-all-start.2 = ((bf16[16,4,128,256]{3,2,1,0:T(8,128)(2,1)}), bf16[16,4,128,256]{3,2,1,0:T(8,128)(2,1)}, u32[]{:S(2)}, u32[]{:S(2)}) async-start(bf16[16,4,128,256]{3,2,1,0:T(8,128)(2,1)} %bitcast.83), calls=%async_computation.2 | async-start | bytes 8388608 | tf_op jit(solution)/shard_map/all_to_all | solution.py:296
  154.8 0.8 convert_reduce_fusion
  155.6 1.0 copy-done.21
  156.6 1.0 convolution_bitcast_fusion
  157.7 0.4 collective-permute-start
  158.1 1.1 collective-permute-done
  159.3 1.9 collective-permute-start.1
  161.2 2.8 %copy-done.5 = bf16[48,4,128,128]{3,2,1,0:T(8,128)(2,1)S(1)} copy-done((bf16[48,4,128,128]{3,2,1,0:T(8,128)(2,1)S(1)}, bf16[48,4,128,128]{3,2,1,0:T(8,128)(2,1)}, u32[]{:S(2)}) %copy-start.5) | copy-done | bytes 6291480
  164.0 1.9 copy-done.14
  165.9 24.8 %local_terms.1.local_ref = f32[48,128,256]{2,1,0:T(8,128)S(1)} custom-call(s32[4,48]{1,0:T(4,128)S(1)} %get-tuple-element.44.rows_index.target_ref, bf16[48,4,128,128]{3,2,1,0:T(8,128)(2,1)S(1)} %copy-done.5, bf16[48,128,256]{2,1,0:T(8,128)(2,1)S(1)} %copy-done.14), custom_call_target="tpu_custom_call" | custom-call | tf_op jit(solution)/shard_map/local_terms/pallas_call | solution.py:239
  190.7 2.6 copy-done
  193.4 2.0 collective-permute-start.2
  195.4 2.8 %collective-permute-start.3 = (f32[24,256]{1,0:T(8,128)S(1)}, f32[24,256]{1,0:T(8,128)S(1)}, u32[]{:S(2)}, u32[]{:S(2)}) collective-permute-start(f32[24,256]{1,0:T(8,128)S(1)} %get-tuple-element.52), channel_id=1, source_target_pairs={{0,8},{1,9},{2,10},{3,11},{4,12},{5,13},{6,14},{7,15},{8,0},{9,1},... | collective-permute-start | bytes 73736 | tf_op jit(solution)/shard_map/ppermute | solution.py:304
  198.2 25.9 %collective-permute-done.2 = f32[24,256]{1,0:T(8,128)S(1)} collective-permute-done((f32[24,256]{1,0:T(8,128)S(1)}, f32[24,256]{1,0:T(8,128)S(1)}, u32[]{:S(2)}, u32[]{:S(2)}) %collective-permute-start.2) | collective-permute-done | bytes 24608 | tf_op jit(solution)/shard_map/ppermute | solution.py:304
  224.0 26.5 %collective-permute-done.3 = f32[24,256]{1,0:T(8,128)S(1)} collective-permute-done((f32[24,256]{1,0:T(8,128)S(1)}, f32[24,256]{1,0:T(8,128)S(1)}, u32[]{:S(2)}, u32[]{:S(2)}) %collective-permute-start.3) | collective-permute-done | bytes 24608 | tf_op jit(solution)/shard_map/ppermute | solution.py:304
  250.6 0.9 collective-permute-start.5
  251.5 1.2 collective-permute-start.6
  252.7 2.4 collective-permute-start.7
  255.0 1.2 collective-permute-done.6
  256.2 2.1 collective-permute-done.7
  258.4 1.4 collective-permute-start.8
  259.8 3.2 %collective-permute-done.8 = f32[96,256]{1,0:T(8,128)S(1)} collective-permute-done((f32[96,256]{1,0:T(8,128)S(1)}, f32[96,256]{1,0:T(8,128)S(1)}, u32[]{:S(2)}, u32[]{:S(2)}) %collective-permute-start.8) | collective-permute-done | bytes 98336 | tf_op jit(solution)/shard_map/ppermute | solution.py:304
  263.3 1.4 collective-permute-done.9
  264.7 0.7 slice.47
  265.4 0.6 slice.48
  266.0 2.8 %copy-done.1 = f32[48,128,256]{2,1,0:T(8,128)S(1)} copy-done((f32[48,128,256]{2,1,0:T(8,128)S(1)}, f32[48,128,256]{2,1,0:T(8,128)}, u32[]{:S(2)}) %copy-start.1) | copy-done | bytes 6291480
  268.8 5.6 %final_sum.1 = bf16[48,128,256]{2,1,0:T(8,128)(2,1)} custom-call(s32[16,128]{1,0:T(8,128)S(1)} %get-tuple-element.27.wanted_ref, f32[48,128,256]{2,1,0:T(8,128)S(1)} %copy-done.1, bf16[64,128,256]{2,1,0:T(8,128)(2,1)} %bitcast.14.returned_ref), custom_call_target="tpu_custom_call" | custom-call | tf_op jit(solution)/shard_map/final_sum/pallas_call | solution.py:278
  (59 shorter events, 0.5 us)
Async XLA Ops:
  2.0 13.9 %all-to-all-start = ((s32[16,1,192]{2,1,0:T(1,128)}), s32[16,1,192]{2,1,0:T(1,128)S(1)}, u32[]{:S(2)}, u32[]{:S(2)}) async-start(s32[16,1,192]{2,1,0:T(1,128)} %broadcast_in_dim.11), calls=%async_computation | async-start | bytes 32768 | tf_op jit(solution)/shard_map/all_to_all | solution.py:336
  15.9 1.9 copy-start.2
  22.7 2.0 copy-start.10
  24.7 4.7 %copy-start.22 = (s32[4,48]{1,0:T(4,128)S(1)}, s32[4,48]{1,0:T(4,128)}, u32[]{:S(2)}) copy-start(s32[4,48]{1,0:T(4,128)} %param.10) | copy-start | bytes 2308
  24.7 20.2 %copy-start.16 = (s32[16,6144]{1,0:T(8,128)S(1)}, s32[16,6144]{1,0:T(8,128)}, u32[]{:S(2)}) copy-start(s32[16,6144]{1,0:T(8,128)} %nbr_ref) | copy-start | bytes 1179652
  24.7 82.2 %copy-start.19 = (f32[256]{0:T(256)S(1)}, f32[256]{0:T(256)}, u32[]{:S(2)}) copy-start(f32[256]{0:T(256)} %param.9) | copy-start | bytes 3076
  24.7 82.2 %all-to-all-start.1 = ((bf16[16,4,128,256]{3,2,1,0:T(8,128)(2,1)}), bf16[16,4,128,256]{3,2,1,0:T(8,128)(2,1)}, u32[]{:S(2)}, u32[]{:S(2)}) async-start(bf16[16,4,128,256]{3,2,1,0:T(8,128)(2,1)} %bitcast.84), calls=%async_computation.1 | async-start | bytes 8388608 | tf_op jit(solution)/shard_map/all_to_all | solution.py:296
  29.4 77.5 %copy-start.3 = (bf16[6144,256]{1,0:T(8,128)(2,1)S(1)}, bf16[6144,256]{1,0:T(8,128)(2,1)}, u32[]{:S(2)}) copy-start(bf16[6144,256]{1,0:T(8,128)(2,1)} %param.7) | copy-start | bytes 9437188
  44.9 1.0 copy-start.17
  71.3 2.6 copy-start.4
  73.9 2.6 copy-start.7
  76.5 30.4 %copy-start.18 = (bf16[256,256]{1,0:T(8,128)(2,1)S(1)}, bf16[256,256]{1,0:T(8,128)(2,1)}, u32[]{:S(2)}) copy-start(bf16[256,256]{1,0:T(8,128)(2,1)} %weight_ref.1) | copy-start | bytes 393220
  106.9 1.6 copy-start.6
  108.5 2.8 %copy-start.8 = (bf16[48,128,512]{2,1,0:T(8,128)(2,1)S(1)}, bf16[48,128,512]{2,1,0:T(8,128)(2,1)}, u32[]{:S(2)}) copy-start(bf16[48,128,512]{2,1,0:T(8,128)(2,1)} %copy-done.7) | copy-start | bytes 18874372
  111.3 1.9 copy-start.15
  127.8 2.1 copy-start.9
  129.9 1.6 copy-start.11
  131.5 1.7 copy-start.13
  133.2 1.6 copy-start.20
  134.8 20.0 %copy-start.12 = (bf16[48,128,256]{2,1,0:T(8,128)(2,1)S(1)}, bf16[48,128,256]{2,1,0:T(8,128)(2,1)}, u32[]{:S(2)}) copy-start(bf16[48,128,256]{2,1,0:T(8,128)(2,1)} %copy-done.11) | copy-start | bytes 9437188
  134.8 131.2 %all-to-all-start.2 = ((bf16[16,4,128,256]{3,2,1,0:T(8,128)(2,1)}), bf16[16,4,128,256]{3,2,1,0:T(8,128)(2,1)}, u32[]{:S(2)}, u32[]{:S(2)}) async-start(bf16[16,4,128,256]{3,2,1,0:T(8,128)(2,1)} %bitcast.83), calls=%async_computation.2 | async-start | bytes 8388608 | tf_op jit(solution)/shard_map/all_to_all | solution.py:296
  154.7 1.9 copy-start.21
  157.7 1.5 collective-permute-start
  159.3 34.1 %collective-permute-start.1 = (f32[96,256]{1,0:T(8,128)S(1)}, f32[96,256]{1,0:T(8,128)S(1)}, u32[]{:S(2)}, u32[]{:S(2)}) collective-permute-start(f32[96,256]{1,0:T(8,128)S(1)} %slice_select_fusion.1), channel_id=1, source_target_pairs={{0,2},{1,3},{2,0},{3,1},{4,6},{5,7},{6,4},{7,5},{8,10},{9,11},{10,... | collective-permute-start | bytes 294920 | tf_op jit(solution)/shard_map/ppermute | solution.py:304
  161.2 2.8 %copy-start.5 = (bf16[48,4,128,128]{3,2,1,0:T(8,128)(2,1)S(1)}, bf16[48,4,128,128]{3,2,1,0:T(8,128)(2,1)}, u32[]{:S(2)}) copy-start(bf16[48,4,128,128]{3,2,1,0:T(8,128)(2,1)} %copy-done.4) | copy-start | bytes 18874372
  164.0 1.9 copy-start.14
  190.7 2.6 copy-start
  193.4 30.6 %collective-permute-start.2 = (f32[24,256]{1,0:T(8,128)S(1)}, f32[24,256]{1,0:T(8,128)S(1)}, u32[]{:S(2)}, u32[]{:S(2)}) collective-permute-start(f32[24,256]{1,0:T(8,128)S(1)} %get-tuple-element.50), channel_id=1, source_target_pairs={{0,4},{1,5},{2,6},{3,7},{4,0},{5,1},{6,2},{7,3},{8,12},{9,13},{10,... | collective-permute-start | bytes 73736 | tf_op jit(solution)/shard_map/ppermute | solution.py:304
  195.4 55.2 %collective-permute-start.3 = (f32[24,256]{1,0:T(8,128)S(1)}, f32[24,256]{1,0:T(8,128)S(1)}, u32[]{:S(2)}, u32[]{:S(2)}) collective-permute-start(f32[24,256]{1,0:T(8,128)S(1)} %get-tuple-element.52), channel_id=1, source_target_pairs={{0,8},{1,9},{2,10},{3,11},{4,12},{5,13},{6,14},{7,15},{8,0},{9,1},... | collective-permute-start | bytes 73736 | tf_op jit(solution)/shard_map/ppermute | solution.py:304
  198.2 52.4 %collective-permute-start.4 = (f32[24,256]{1,0:T(8,128)S(1)}, f32[24,256]{1,0:T(8,128)S(1)}, u32[]{:S(2)}, u32[]{:S(2)}) collective-permute-start(f32[24,256]{1,0:T(8,128)S(1)} %get-tuple-element.51), channel_id=1, source_target_pairs={{0,12},{1,13},{2,14},{3,15},{4,8},{5,9},{6,10},{7,11},{8,4},{9,5},... | collective-permute-start | bytes 73736 | tf_op jit(solution)/shard_map/ppermute | solution.py:304
  250.6 4.5 %collective-permute-start.5 = (f32[24,256]{1,0:T(8,128)S(1)}, f32[24,256]{1,0:T(8,128)S(1)}, u32[]{:S(2)}, u32[]{:S(2)}) collective-permute-start(f32[24,256]{1,0:T(8,128)S(1)} %fusion.2), channel_id=1, source_target_pairs={{0,4},{1,5},{2,6},{3,7},{4,0},{5,1},{6,2},{7,3},{8,12},{9,13},{10,... | collective-permute-start | bytes 73736 | tf_op jit(solution)/shard_map/ppermute | solution.py:304
  251.5 4.7 %collective-permute-start.6 = (f32[24,256]{1,0:T(8,128)S(1)}, f32[24,256]{1,0:T(8,128)S(1)}, u32[]{:S(2)}, u32[]{:S(2)}) collective-permute-start(f32[24,256]{1,0:T(8,128)S(1)} %fusion.2), channel_id=1, source_target_pairs={{0,8},{1,9},{2,10},{3,11},{4,12},{5,13},{6,14},{7,15},{8,0},{9,1},... | collective-permute-start | bytes 73736 | tf_op jit(solution)/shard_map/ppermute | solution.py:304
  252.7 5.6 %collective-permute-start.7 = (f32[24,256]{1,0:T(8,128)S(1)}, f32[24,256]{1,0:T(8,128)S(1)}, u32[]{:S(2)}, u32[]{:S(2)}) collective-permute-start(f32[24,256]{1,0:T(8,128)S(1)} %fusion.2), channel_id=1, source_target_pairs={{0,12},{1,13},{2,14},{3,15},{4,8},{5,9},{6,10},{7,11},{8,4},{9,5},... | collective-permute-start | bytes 73736 | tf_op jit(solution)/shard_map/ppermute | solution.py:304
  258.4 4.7 %collective-permute-start.8 = (f32[96,256]{1,0:T(8,128)S(1)}, f32[96,256]{1,0:T(8,128)S(1)}, u32[]{:S(2)}, u32[]{:S(2)}) collective-permute-start(f32[96,256]{1,0:T(8,128)S(1)} %pad_maximum_fusion.2), channel_id=1, source_target_pairs={{0,2},{1,3},{2,0},{3,1},{4,6},{5,7},{6,4},{7,5},{8,10},{9,11},{10,... | collective-permute-start | bytes 294920 | tf_op jit(solution)/shard_map/ppermute | solution.py:304
  263.2 1.5 collective-permute-start.9
  266.0 2.8 %copy-start.1 = (f32[48,128,256]{2,1,0:T(8,128)S(1)}, f32[48,128,256]{2,1,0:T(8,128)}, u32[]{:S(2)}) copy-start(f32[48,128,256]{2,1,0:T(8,128)} %copy-done) | copy-start | bytes 18874372

commit v3 on v2

--- a/solution.py
+++ b/solution.py
@@ -15,7 +15,7 @@
 SMEM = pltpu.MemorySpace.SMEM
 HBM = pltpu.MemorySpace.HBM
 PIECE = 32
-MIDDLE_VMEM = 20 << 20
+MIDDLE_VMEM = 32 << 20
 
 
 def whole(space=VMEM):
@@ -124,7 +124,8 @@
 
 def middle_kernel(
     rows_index, term_tile, rows_ref, sent_ref, x_ref, arrived_ref, weight_ref, bias_ref, cot_ref,
-    out_ref, agg_ref, pg_ref, grad_ref, terms_ref, near, terms, pre, near_sems, sems,
+    out_hbm, agg_hbm, pg_hbm, grad_hbm, terms_ref, near, terms, pre, out_ref, agg_ref, pg_ref, grad_ref,
+    near_sems, sems, store_sems,
 ):
     tile_count = x_ref.shape[0]
     slots = arrived_ref.shape[0]
@@ -137,6 +138,14 @@
     others.wait()
     weight = weight_ref[...]
     bias = bias_ref[...]
+    results = ((out_ref, out_hbm), (agg_ref, agg_hbm), (pg_ref, pg_hbm), (grad_ref, grad_hbm))
+
+    def stores(step):
+        part = pl.ds(step * group, group)
+        return [
+            pltpu.make_async_copy(held.at[part], target.at[part], store_sems.at[which, step])
+            for which, (held, target) in enumerate(results)
+        ]
 
     def group_step(step, carry):
         start = step * group
@@ -163,6 +172,8 @@
             preact_grad, weight, (((1,), (1,)), ((), ())), preferred_element_type=jnp.float32
         )
         grad_ref[pl.ds(start, group)] = gradient.astype(jnp.bfloat16).reshape(group, TILE, C)
+        for store in stores(step):
+            store.start()
         return carry
 
     lax.fori_loop(0, tile_count // group, group_step, 0)
@@ -187,6 +198,9 @@
         return carry
 
     lax.fori_loop(0, sems.shape[0], finish, 0)
+    for step in range(tile_count // group):
+        for store in stores(step):
+            store.wait()
 
 
 def middle(rows_index, term_tile, rows, sent, x_tiles, arrived, weight, bias, cot, devices):
@@ -198,14 +212,16 @@
         middle_kernel,
         name="middle",
         in_specs=[whole(SMEM)] * 2 + [whole()] * 3 + [whole(HBM)] + [whole()] * 3,
-        out_specs=[whole()] * 4 + [whole(HBM)],
+        out_specs=[whole(HBM)] * 5,
         out_shape=[tiles] * 4 + [jax.ShapeDtypeStruct((slots, TILE, C), jnp.bfloat16)],
         scratch_shapes=[
             pltpu.VMEM((tile_count + slots, TILE, C), jnp.bfloat16),
             pltpu.VMEM((slots, TILE, C), jnp.bfloat16),
             pltpu.VMEM((group * TILE, C), jnp.float32),
+            *[pltpu.VMEM(tiles.shape, tiles.dtype) for _ in range(4)],
             pltpu.SemaphoreType.DMA((2,)),
             pltpu.SemaphoreType.DMA((devices,)),
+            pltpu.SemaphoreType.DMA((4, tile_count // group)),
         ],
         compiler_params=pltpu.CompilerParams(vmem_limit_bytes=MIDDLE_VMEM),
     )(rows_index, term_tile, rows, sent, x_tiles, arrived, weight, bias, cot)
@@ -296,7 +312,7 @@
     return lax.all_to_all(parted, GROUP, split_axis=0, concat_axis=0, tiled=True).reshape(array.shape)
 
 
-def group_sum(part, devices, position, hold):
+def group_sum(part, devices, position, hold, hold_last):
     bits = devices.bit_length() - 1
     low = bits - 2
 
@@ -315,7 +331,7 @@
     place = position >> low
     got = [swap(lax.dynamic_index_in_dim(quarters, place ^ r, 0, False), r << low) for r in range(1, 4)]
     part = lax.dynamic_index_in_dim(quarters, place, 0, False) + got[0] + got[1] + got[2]
-    gathered = jnp.stack([part] + [swap(part, r << low) for r in range(1, 4)])
+    gathered = jnp.stack([part] + hold_last([swap(part, r << low) for r in range(1, 4)]))
     part = jnp.concatenate([lax.dynamic_index_in_dim(gathered, place ^ j, 0, False) for j in range(4)])
     for bit in reversed(range(low)):
         upper = (position >> bit) & 1 == 1
@@ -378,10 +394,16 @@
     bias_part = jnp.sum(preact_grad.astype(jnp.float32), axis=0)
     part = jnp.concatenate([weight_part, jnp.broadcast_to(bias_part[None], (C // 2, C))])
     local = local_terms(rows_index, columns, gradient)
-    summed = group_sum(part, devices, position, lambda got: lax.optimization_barrier((got, local))[0])
+    grad_features = final_sum(wanted, local, returned, devices)
+    summed = group_sum(
+        part,
+        devices,
+        position,
+        lambda got: lax.optimization_barrier((got, local))[0],
+        lambda got: lax.optimization_barrier((got, grad_features))[0],
+    )
     normalizer = 1.0 / math.sqrt(features.shape[0] * devices)
     summed = summed * normalizer
-    grad_features = final_sum(wanted, local, returned, devices)
     return (out.reshape(-1, C), grad_features.reshape(-1, C), summed[:C], summed[C])
 
 

time: 276 us -> 271 us (0.982)
  waiting for transfers between devices: 92.5 us -> 89.6 us
  local copies, waits for them, and re-layouts: 49.3 us -> 46.5 us
    ppermute x10, waiting for transfers between devices: 61.4 us -> 58.4 us  [swap(): lax.ppermute(piece, GROUP, [(d, d ^ difference) for d in range(devices)])]
    unnamed x54 -> x52, local copies, waits for them, and re-layouts: 34.5 us -> 31.7 us
  transfers between devices with their start and end apart: 13 -> 13, of which waited for: 9 -> 7; matrix products, arithmetic and copies ran while one was open for 9% -> 9% of each run, Pallas kernels for 18% -> 21%
where the time goes in v3:
time: 271 us; the launch traced here: 270 us
  waiting for transfers between devices  89.6 us (33%)
  Pallas kernels  76.1 us (28%)
  local copies, waits for them, and re-layouts  46.5 us (17%)
  starting transfers between devices  45.1 us (17%)
  other arithmetic  10.1 us (4%)
    ppermute x10, waiting for transfers between devices, swap(): lax.ppermute(piece, GROUP, [(d, d ^ difference) for d in range(devices)])  58.4 us
    unnamed x52, local copies, waits for them, and re-layouts  31.7 us
    pallas_call x1, Pallas kernels, build_blocks(): pl.pallas_call(blocks_kernel, name='blocks', grid=(tile_count,), in_specs...  25.3 us
    all_to_all x2, waiting for transfers between devices, exchange(): lax.all_to_all(parted, GROUP, split_axis=0, concat_axis=0, tiled=True)  24.7 us
    all_to_all x2, starting transfers between devices, exchange(): lax.all_to_all(parted, GROUP, split_axis=0, concat_axis=0, tiled=True)  24.6 us
    pallas_call x1, Pallas kernels, local_terms(): pl.pallas_call(local_kernel, name='local_terms', in_specs=[whole(SMEM), w...  24.5 us
    pallas_call x1, Pallas kernels, middle(): pl.pallas_call(middle_kernel, name='middle', in_specs=[whole(SMEM)] * 2 +...  16.1 us
    ppermute x10, starting transfers between devices, swap(): lax.ppermute(piece, GROUP, [(d, d ^ difference) for d in range(devices)])  13.1 us
  transfers between devices with their start and end apart: 13, of which 7 were waited for; matrix products, arithmetic and copies ran while one was open for 9% of the time, Pallas kernels for 21%

profile of v3, /device:TPU:0, one launch (start us, length us, event | category | flops | bytes accessed | tf_op | source)
XLA Modules:
  0.0 269.5 jit_solution(7342070131793762206)
XLA Ops:
  0.6 0.8 broadcast_in_dim.10
  1.4 0.6 broadcast_in_dim.11
  2.0 7.4 %all-to-all-start = ((s32[16,1,192]{2,1,0:T(1,128)}), s32[16,1,192]{2,1,0:T(1,128)S(1)}, u32[]{:S(2)}, u32[]{:S(2)}) async-start(s32[16,1,192]{2,1,0:T(1,128)} %broadcast_in_dim.11), calls=%async_computation | async-start | bytes 32768 | tf_op jit(solution)/shard_map/all_to_all | solution.py:352
  9.4 6.5 %all-to-all-done = s32[16,1,192]{2,1,0:T(1,128)S(1)} async-done(((s32[16,1,192]{2,1,0:T(1,128)}), s32[16,1,192]{2,1,0:T(1,128)S(1)}, u32[]{:S(2)}, u32[]{:S(2)}) %all-to-all-start) | async-done | bytes 12320 | tf_op jit(solution)/shard_map/all_to_all | solution.py:352
  15.9 1.9 copy-done.2
  17.8 4.6 %pack.1 = (bf16[64,128,256]{2,1,0:T(8,128)(2,1)S(1)}, s32[16,128]{1,0:T(8,128)S(1)}) custom-call(s32[1]{0:T(128)} %bitcast.position_ref, s32[16,192]{1,0:T(8,128)S(1)} %bitcast.86, bf16[48,128,256]{2,1,0:T(8,128)(2,1)S(1)} %bitcast.80), custom_call_target="tpu_custom_call" | custom-call | tf_op jit(solution)/shard_map/pack/pallas_call | solution.py:72
  22.4 2.0 copy-done.9
  24.4 4.7 %all-to-all-start.1 = ((bf16[16,4,128,256]{3,2,1,0:T(8,128)(2,1)}), bf16[16,4,128,256]{3,2,1,0:T(8,128)(2,1)}, u32[]{:S(2)}, u32[]{:S(2)}) async-start(bf16[16,4,128,256]{3,2,1,0:T(8,128)(2,1)} %bitcast.84), calls=%async_computation.1 | async-start | bytes 8388608 | tf_op jit(solution)/shard_map/all_to_all | solution.py:312
  29.1 0.0 copy-start.3
  29.1 0.6 broadcast_compare_fusion
  29.7 1.1 eq.49
  30.8 1.3 and.58
  32.1 0.6 fusion.6
  32.7 0.6 copy_bitcast_fusion
  33.3 1.9 reduce-window.6
  35.1 1.5 slice_reduce_fusion
  36.6 1.3 reduce-window.9
  37.9 0.7 slice.32
  38.6 0.8 bitcast_bitcast_fusion
  39.3 1.2 fusion.4
  40.5 1.3 reshape.139
  41.9 1.3 fusion.7
  43.2 1.3 eq.56
  44.5 1.0 copy-done.16
  45.5 25.3 %blocks.1 = (bf16[48,128,512]{2,1,0:T(8,128)(2,1)S(1)}, bf16[48,4,128,128]{3,2,1,0:T(8,128)(2,1)S(1)}) custom-call(s32[16,6144]{1,0:T(8,128)S(1)} %copy-done.15, s32[16,6144]{1,0:T(8,128)S(1)} %copy-done.16), custom_call_target="tpu_custom_call" | custom-call | tf_op jit(solution)/shard_map/blocks/pallas_call | solution.py:108
  70.8 2.6 copy-done.4
  73.4 2.6 copy-done.7
  76.1 0.8 select_reduce_fusion
  76.9 4.9 %gather_fusion = bf16[64,128,128]{2,1,0:T(8,128)(2,1)} fusion(bf16[192,128,128]{2,1,0:T(8,128)(2,1)} %bitcast.82, s32[1024]{0:T(1024)S(1)} %pad_clamp_fusion), kind=kCustom, calls=%fused_computation | custom fusion | bytes 4194560 | tf_op jit(solution)/shard_map/gather | solution.py:380
  81.9 24.7 %all-to-all-done.1 = bf16[16,4,128,256]{3,2,1,0:T(8,128)(2,1)} async-done(((bf16[16,4,128,256]{3,2,1,0:T(8,128)(2,1)}), bf16[16,4,128,256]{3,2,1,0:T(8,128)(2,1)}, u32[]{:S(2)}, u32[]{:S(2)}) %all-to-all-start.1) | async-done | bytes 4194336 | tf_op jit(solution)/shard_map/all_to_all | solution.py:312
  106.6 1.6 copy-done.6
  108.2 1.9 copy-done.14
  110.1 16.1 %middle.1 = (bf16[48,128,256]{2,1,0:T(8,128)(2,1)}, bf16[48,128,256]{2,1,0:T(8,128)(2,1)S(1)}, bf16[48,128,256]{2,1,0:T(8,128)(2,1)S(1)}, bf16[48,128,256]{2,1,0:T(8,128)(2,1)S(1)}, bf16[64,128,256]{2,1,0:T(8,128)(2,1)S(1)}) custom-call(s32[4,48]{1,0:T(4,128)S(1)} %get-tuple-element.50.rows_index.target_ref, s32[64]{0:T(128)S(1)} %and_select_fusion.1.term_tile, ...), custom_call_target="tpu_custom_call" | custom-call | tf_op jit(solution)/shard_map/middle/pallas_call | solution.py:211
  126.2 2.1 copy-done.8
  128.2 1.6 copy-done.10
  129.8 1.7 copy-done.12
  131.5 1.6 copy-done.19
  133.1 19.9 %all-to-all-start.2 = ((bf16[16,4,128,256]{3,2,1,0:T(8,128)(2,1)}), bf16[16,4,128,256]{3,2,1,0:T(8,128)(2,1)}, u32[]{:S(2)}, u32[]{:S(2)}) async-start(bf16[16,4,128,256]{3,2,1,0:T(8,128)(2,1)} %bitcast.83), calls=%async_computation.2 | async-start | bytes 8388608 | tf_op jit(solution)/shard_map/all_to_all | solution.py:312
  153.1 0.8 convert_reduce_fusion
  153.9 1.0 copy-done.20
  155.0 1.0 convolution_bitcast_fusion
  156.0 0.4 collective-permute-start
  156.5 1.1 collective-permute-done
  157.6 1.9 collective-permute-start.1
  159.6 2.8 %copy-done.5 = bf16[48,4,128,128]{3,2,1,0:T(8,128)(2,1)S(1)} copy-done((bf16[48,4,128,128]{3,2,1,0:T(8,128)(2,1)S(1)}, bf16[48,4,128,128]{3,2,1,0:T(8,128)(2,1)}, u32[]{:S(2)}) %copy-start.5) | copy-done | bytes 6291480
  162.3 1.9 copy-done.13
  164.2 24.5 %local_terms.1.local_ref = f32[48,128,256]{2,1,0:T(8,128)S(1)} custom-call(s32[4,48]{1,0:T(4,128)S(1)} %get-tuple-element.50.rows_index.target_ref, bf16[48,4,128,128]{3,2,1,0:T(8,128)(2,1)S(1)} %copy-done.5, bf16[48,128,256]{2,1,0:T(8,128)(2,1)S(1)} %copy-done.13), custom_call_target="tpu_custom_call" | custom-call | tf_op jit(solution)/shard_map/local_terms/pallas_call | solution.py:255
  188.8 2.6 copy-done
  191.5 2.3 collective-permute-start.2
  193.7 1.1 collective-permute-start.3
  194.8 1.4 collective-permute-start.4
  196.2 26.2 %collective-permute-done.2 = f32[24,256]{1,0:T(8,128)S(1)} collective-permute-done((f32[24,256]{1,0:T(8,128)S(1)}, f32[24,256]{1,0:T(8,128)S(1)}, u32[]{:S(2)}, u32[]{:S(2)}) %collective-permute-start.2) | collective-permute-done | bytes 24608 | tf_op jit(solution)/shard_map/ppermute | solution.py:320
  222.4 26.5 %collective-permute-done.3 = f32[24,256]{1,0:T(8,128)S(1)} collective-permute-done((f32[24,256]{1,0:T(8,128)S(1)}, f32[24,256]{1,0:T(8,128)S(1)}, u32[]{:S(2)}, u32[]{:S(2)}) %collective-permute-start.3) | collective-permute-done | bytes 24608 | tf_op jit(solution)/shard_map/ppermute | solution.py:320
  248.9 0.9 collective-permute-start.5
  249.8 1.2 collective-permute-start.6
  251.0 2.4 collective-permute-start.7
  253.4 2.8 %copy-done.1 = f32[48,128,256]{2,1,0:T(8,128)S(1)} copy-done((f32[48,128,256]{2,1,0:T(8,128)S(1)}, f32[48,128,256]{2,1,0:T(8,128)}, u32[]{:S(2)}) %copy-start.1) | copy-done | bytes 6291480
  256.1 5.6 %final_sum.1 = bf16[48,128,256]{2,1,0:T(8,128)(2,1)} custom-call(s32[16,128]{1,0:T(8,128)S(1)} %get-tuple-element.30.wanted_ref, f32[48,128,256]{2,1,0:T(8,128)S(1)} %copy-done.1, bf16[64,128,256]{2,1,0:T(8,128)(2,1)} %bitcast.14.returned_ref), custom_call_target="tpu_custom_call" | custom-call | tf_op jit(solution)/shard_map/final_sum/pallas_call | solution.py:294
  261.9 1.5 collective-permute-start.8
  263.4 3.2 %collective-permute-done.8 = f32[96,256]{1,0:T(8,128)S(1)} collective-permute-done((f32[96,256]{1,0:T(8,128)S(1)}, f32[96,256]{1,0:T(8,128)S(1)}, u32[]{:S(2)}, u32[]{:S(2)}) %collective-permute-start.8) | collective-permute-done | bytes 98336 | tf_op jit(solution)/shard_map/ppermute | solution.py:320
  266.7 0.1 collective-permute-start.9
  266.8 1.4 collective-permute-done.9
  268.2 0.7 slice.47
  269.0 0.6 slice.48
  (57 shorter events, 0.4 us)
Async XLA Ops:
  2.0 13.9 %all-to-all-start = ((s32[16,1,192]{2,1,0:T(1,128)}), s32[16,1,192]{2,1,0:T(1,128)S(1)}, u32[]{:S(2)}, u32[]{:S(2)}) async-start(s32[16,1,192]{2,1,0:T(1,128)} %broadcast_in_dim.11), calls=%async_computation | async-start | bytes 32768 | tf_op jit(solution)/shard_map/all_to_all | solution.py:352
  15.9 1.9 copy-start.2
  22.4 2.0 copy-start.9
  24.4 4.7 %copy-start.21 = (s32[4,48]{1,0:T(4,128)S(1)}, s32[4,48]{1,0:T(4,128)}, u32[]{:S(2)}) copy-start(s32[4,48]{1,0:T(4,128)} %param.10) | copy-start | bytes 2308
  24.4 20.1 %copy-start.15 = (s32[16,6144]{1,0:T(8,128)S(1)}, s32[16,6144]{1,0:T(8,128)}, u32[]{:S(2)}) copy-start(s32[16,6144]{1,0:T(8,128)} %nbr_ref) | copy-start | bytes 1179652
  24.4 82.2 %copy-start.18 = (f32[256]{0:T(256)S(1)}, f32[256]{0:T(256)}, u32[]{:S(2)}) copy-start(f32[256]{0:T(256)} %param.9) | copy-start | bytes 3076
  24.4 82.2 %all-to-all-start.1 = ((bf16[16,4,128,256]{3,2,1,0:T(8,128)(2,1)}), bf16[16,4,128,256]{3,2,1,0:T(8,128)(2,1)}, u32[]{:S(2)}, u32[]{:S(2)}) async-start(bf16[16,4,128,256]{3,2,1,0:T(8,128)(2,1)} %bitcast.84), calls=%async_computation.1 | async-start | bytes 8388608 | tf_op jit(solution)/shard_map/all_to_all | solution.py:312
  29.1 77.5 %copy-start.3 = (bf16[6144,256]{1,0:T(8,128)(2,1)S(1)}, bf16[6144,256]{1,0:T(8,128)(2,1)}, u32[]{:S(2)}) copy-start(bf16[6144,256]{1,0:T(8,128)(2,1)} %param.7) | copy-start | bytes 9437188
  44.5 1.0 copy-start.16
  70.8 2.6 copy-start.4
  73.4 2.6 copy-start.7
  76.1 30.5 %copy-start.17 = (bf16[256,256]{1,0:T(8,128)(2,1)S(1)}, bf16[256,256]{1,0:T(8,128)(2,1)}, u32[]{:S(2)}) copy-start(bf16[256,256]{1,0:T(8,128)(2,1)} %weight_ref.1) | copy-start | bytes 393220
  106.6 1.6 copy-start.6
  108.2 1.9 copy-start.14
  126.2 2.1 copy-start.8
  128.2 1.6 copy-start.10
  129.8 1.7 copy-start.12
  131.5 1.6 copy-start.19
  133.1 20.0 %copy-start.11 = (bf16[48,128,256]{2,1,0:T(8,128)(2,1)S(1)}, bf16[48,128,256]{2,1,0:T(8,128)(2,1)}, u32[]{:S(2)}) copy-start(bf16[48,128,256]{2,1,0:T(8,128)(2,1)} %copy-done.10) | copy-start | bytes 9437188
  133.1 120.2 %all-to-all-start.2 = ((bf16[16,4,128,256]{3,2,1,0:T(8,128)(2,1)}), bf16[16,4,128,256]{3,2,1,0:T(8,128)(2,1)}, u32[]{:S(2)}, u32[]{:S(2)}) async-start(bf16[16,4,128,256]{3,2,1,0:T(8,128)(2,1)} %bitcast.83), calls=%async_computation.2 | async-start | bytes 8388608 | tf_op jit(solution)/shard_map/all_to_all | solution.py:312
  153.1 1.9 copy-start.20
  156.0 1.5 collective-permute-start
  157.6 33.8 %collective-permute-start.1 = (f32[96,256]{1,0:T(8,128)S(1)}, f32[96,256]{1,0:T(8,128)S(1)}, u32[]{:S(2)}, u32[]{:S(2)}) collective-permute-start(f32[96,256]{1,0:T(8,128)S(1)} %slice_select_fusion.1), channel_id=1, source_target_pairs={{0,2},{1,3},{2,0},{3,1},{4,6},{5,7},{6,4},{7,5},{8,10},{9,11},{10,... | collective-permute-start | bytes 294920 | tf_op jit(solution)/shard_map/ppermute | solution.py:320
  159.6 2.8 %copy-start.5 = (bf16[48,4,128,128]{3,2,1,0:T(8,128)(2,1)S(1)}, bf16[48,4,128,128]{3,2,1,0:T(8,128)(2,1)}, u32[]{:S(2)}) copy-start(bf16[48,4,128,128]{3,2,1,0:T(8,128)(2,1)} %copy-done.4) | copy-start | bytes 18874372
  162.3 1.9 copy-start.13
  188.8 2.6 copy-start
  191.5 30.9 %collective-permute-start.2 = (f32[24,256]{1,0:T(8,128)S(1)}, f32[24,256]{1,0:T(8,128)S(1)}, u32[]{:S(2)}, u32[]{:S(2)}) collective-permute-start(f32[24,256]{1,0:T(8,128)S(1)} %get-tuple-element.56), channel_id=1, source_target_pairs={{0,4},{1,5},{2,6},{3,7},{4,0},{5,1},{6,2},{7,3},{8,12},{9,13},{10,... | collective-permute-start | bytes 73736 | tf_op jit(solution)/shard_map/ppermute | solution.py:320
  193.7 55.2 %collective-permute-start.3 = (f32[24,256]{1,0:T(8,128)S(1)}, f32[24,256]{1,0:T(8,128)S(1)}, u32[]{:S(2)}, u32[]{:S(2)}) collective-permute-start(f32[24,256]{1,0:T(8,128)S(1)} %get-tuple-element.58), channel_id=1, source_target_pairs={{0,8},{1,9},{2,10},{3,11},{4,12},{5,13},{6,14},{7,15},{8,0},{9,1},... | collective-permute-start | bytes 73736 | tf_op jit(solution)/shard_map/ppermute | solution.py:320
  194.8 54.1 %collective-permute-start.4 = (f32[24,256]{1,0:T(8,128)S(1)}, f32[24,256]{1,0:T(8,128)S(1)}, u32[]{:S(2)}, u32[]{:S(2)}) collective-permute-start(f32[24,256]{1,0:T(8,128)S(1)} %get-tuple-element.57), channel_id=1, source_target_pairs={{0,12},{1,13},{2,14},{3,15},{4,8},{5,9},{6,10},{7,11},{8,4},{9,5},... | collective-permute-start | bytes 73736 | tf_op jit(solution)/shard_map/ppermute | solution.py:320
  248.9 12.9 %collective-permute-start.5 = (f32[24,256]{1,0:T(8,128)S(1)}, f32[24,256]{1,0:T(8,128)S(1)}, u32[]{:S(2)}, u32[]{:S(2)}) collective-permute-start(f32[24,256]{1,0:T(8,128)S(1)} %fusion.2), channel_id=1, source_target_pairs={{0,4},{1,5},{2,6},{3,7},{4,0},{5,1},{6,2},{7,3},{8,12},{9,13},{10,... | collective-permute-start | bytes 73736 | tf_op jit(solution)/shard_map/ppermute | solution.py:320
  249.8 12.0 %collective-permute-start.6 = (f32[24,256]{1,0:T(8,128)S(1)}, f32[24,256]{1,0:T(8,128)S(1)}, u32[]{:S(2)}, u32[]{:S(2)}) collective-permute-start(f32[24,256]{1,0:T(8,128)S(1)} %fusion.2), channel_id=1, source_target_pairs={{0,8},{1,9},{2,10},{3,11},{4,12},{5,13},{6,14},{7,15},{8,0},{9,1},... | collective-permute-start | bytes 73736 | tf_op jit(solution)/shard_map/ppermute | solution.py:320
  251.0 10.8 %collective-permute-start.7 = (f32[24,256]{1,0:T(8,128)S(1)}, f32[24,256]{1,0:T(8,128)S(1)}, u32[]{:S(2)}, u32[]{:S(2)}) collective-permute-start(f32[24,256]{1,0:T(8,128)S(1)} %fusion.2), channel_id=1, source_target_pairs={{0,12},{1,13},{2,14},{3,15},{4,8},{5,9},{6,10},{7,11},{8,4},{9,5},... | collective-permute-start | bytes 73736 | tf_op jit(solution)/shard_map/ppermute | solution.py:320
  253.4 2.8 %copy-start.1 = (f32[48,128,256]{2,1,0:T(8,128)S(1)}, f32[48,128,256]{2,1,0:T(8,128)}, u32[]{:S(2)}) copy-start(f32[48,128,256]{2,1,0:T(8,128)} %copy-done) | copy-start | bytes 18874372
  261.9 4.7 %collective-permute-start.8 = (f32[96,256]{1,0:T(8,128)S(1)}, f32[96,256]{1,0:T(8,128)S(1)}, u32[]{:S(2)}, u32[]{:S(2)}) collective-permute-start(f32[96,256]{1,0:T(8,128)S(1)} %pad_maximum_fusion.2), channel_id=1, source_target_pairs={{0,2},{1,3},{2,0},{3,1},{4,6},{5,7},{6,4},{7,5},{8,10},{9,11},{10,... | collective-permute-start | bytes 294920 | tf_op jit(solution)/shard_map/ppermute | solution.py:320
  266.7 1.5 collective-permute-start.9

commit v4 on v3

--- a/solution.py
+++ b/solution.py
@@ -75,7 +75,7 @@
         in_specs=[whole(SMEM), whole(), whole(HBM)],
         out_specs=[whole(HBM), whole()],
         out_shape=[
-            jax.ShapeDtypeStruct((devices * capacity, TILE, C), jnp.bfloat16),
+            HBM((devices * capacity, TILE, C), jnp.bfloat16),
             jax.ShapeDtypeStruct((devices, 128), jnp.int32),
         ],
         scratch_shapes=[
@@ -86,7 +86,7 @@
             pltpu.SemaphoreType.DMA((devices * capacity,)),
         ],
         compiler_params=pltpu.CompilerParams(vmem_limit_bytes=16 << 20),
-    )(position, table, x_tiles)
+    )(position, table, pltpu.with_memory_space_constraint(x_tiles, HBM))
 
 
 def blocks_kernel(nbr_ref, count_ref, rows_ref, columns_ref):
@@ -207,13 +207,13 @@
     tile_count = x_tiles.shape[0]
     slots = arrived.shape[0]
     group = math.gcd(tile_count, 8)
-    tiles = jax.ShapeDtypeStruct((tile_count, TILE, C), jnp.bfloat16)
+    tiles = HBM((tile_count, TILE, C), jnp.bfloat16)
     return pl.pallas_call(
         middle_kernel,
         name="middle",
         in_specs=[whole(SMEM)] * 2 + [whole()] * 3 + [whole(HBM)] + [whole()] * 3,
         out_specs=[whole(HBM)] * 5,
-        out_shape=[tiles] * 4 + [jax.ShapeDtypeStruct((slots, TILE, C), jnp.bfloat16)],
+        out_shape=[tiles] * 4 + [HBM((slots, TILE, C), jnp.bfloat16)],
         scratch_shapes=[
             pltpu.VMEM((tile_count + slots, TILE, C), jnp.bfloat16),
             pltpu.VMEM((slots, TILE, C), jnp.bfloat16),
@@ -257,7 +257,7 @@
         name="local_terms",
         in_specs=[whole(SMEM), whole(), whole()],
         out_specs=whole(),
-        out_shape=jax.ShapeDtypeStruct(grad.shape, jnp.float32),
+        out_shape=HBM(grad.shape, jnp.float32),
         compiler_params=pltpu.CompilerParams(vmem_limit_bytes=24 << 20),
     )(rows_index, columns, grad)
 
@@ -304,7 +304,7 @@
             pltpu.SemaphoreType.DMA((devices,)),
         ],
         compiler_params=pltpu.CompilerParams(vmem_limit_bytes=24 << 20),
-    )(wanted, local, returned)
+    )(wanted, pltpu.with_memory_space_constraint(local, HBM), returned)
 
 
 def exchange(array, devices):

time: 271 us -> 259 us (0.956)
  local copies, waits for them, and re-layouts: 46.5 us -> 31.9 us
  waiting for transfers between devices: 89.6 us -> 86.5 us
    unnamed x52 -> x42, local copies, waits for them, and re-layouts: 31.7 us -> 17.1 us
    pallas_call x1, Pallas kernels: 24.5 us -> 27.8 us  [local_terms(): pl.pallas_call(local_kernel, name='local_terms', in_specs=[whole(SMEM), w...]
    ppermute x10, waiting for transfers between devices: 58.4 us -> 55.5 us  [swap(): lax.ppermute(piece, GROUP, [(d, d ^ difference) for d in range(devices)])]
  transfers between devices with their start and end apart: 13 -> 13, of which waited for: 7 -> 7; matrix products, arithmetic and copies ran while one was open for 9% -> 10% of each run, Pallas kernels for 21% -> 24%
where the time goes in v4:
time: 259 us; the launch traced here: 258 us
  waiting for transfers between devices  86.5 us (33%)
  Pallas kernels  78.4 us (30%)
  starting transfers between devices  45 us (17%)
  local copies, waits for them, and re-layouts  31.9 us (12%)
  other arithmetic  11.9 us (5%)
  matrix products  3.05 us (1%)
    ppermute x10, waiting for transfers between devices, swap(): lax.ppermute(piece, GROUP, [(d, d ^ difference) for d in range(devices)])  55.5 us
    pallas_call x1, Pallas kernels, local_terms(): pl.pallas_call(local_kernel, name='local_terms', in_specs=[whole(SMEM), w...  27.8 us
    pallas_call x1, Pallas kernels, build_blocks(): pl.pallas_call(blocks_kernel, name='blocks', grid=(tile_count,), in_specs...  25.3 us
    all_to_all x2, starting transfers between devices, exchange(): lax.all_to_all(parted, GROUP, split_axis=0, concat_axis=0, tiled=True)  24.6 us
    all_to_all x2, waiting for transfers between devices, exchange(): lax.all_to_all(parted, GROUP, split_axis=0, concat_axis=0, tiled=True)  24.5 us
    unnamed x42, local copies, waits for them, and re-layouts  17.1 us
    pallas_call x1, Pallas kernels, middle(): pl.pallas_call(middle_kernel, name='middle', in_specs=[whole(SMEM)] * 2 +...  13.4 us
    ppermute x10, starting transfers between devices, swap(): lax.ppermute(piece, GROUP, [(d, d ^ difference) for d in range(devices)])  13 us
  transfers between devices with their start and end apart: 13, of which 7 were waited for; matrix products, arithmetic and copies ran while one was open for 10% of the time, Pallas kernels for 24%

profile of v4, /device:TPU:0, one launch (start us, length us, event | category | flops | bytes accessed | tf_op | source)
XLA Modules:
  0.0 257.8 jit_solution(11120409803982236318)
XLA Ops:
  0.6 0.8 broadcast_in_dim.10
  1.4 0.6 broadcast_in_dim.11
  2.0 7.4 %all-to-all-start = ((s32[16,1,192]{2,1,0:T(1,128)}), s32[16,1,192]{2,1,0:T(1,128)S(1)}, u32[]{:S(2)}, u32[]{:S(2)}) async-start(s32[16,1,192]{2,1,0:T(1,128)} %broadcast_in_dim.11), calls=%async_computation | async-start | bytes 32768 | tf_op jit(solution)/shard_map/all_to_all | solution.py:352
  9.4 6.5 %all-to-all-done = s32[16,1,192]{2,1,0:T(1,128)S(1)} async-done(((s32[16,1,192]{2,1,0:T(1,128)}), s32[16,1,192]{2,1,0:T(1,128)S(1)}, u32[]{:S(2)}, u32[]{:S(2)}) %all-to-all-start) | async-done | bytes 12320 | tf_op jit(solution)/shard_map/all_to_all | solution.py:352
  15.9 4.0 %pack.1 = (bf16[64,128,256]{2,1,0:T(8,128)(2,1)}, s32[16,128]{1,0:T(8,128)S(1)}) custom-call(s32[1]{0:T(128)} %bitcast.position_ref, s32[16,192]{1,0:T(8,128)S(1)} %bitcast.84, bf16[48,128,256]{2,1,0:T(8,128)(2,1)} %bitcast.80), custom_call_target="tpu_custom_call" | custom-call | tf_op jit(solution)/shard_map/pack/pallas_call | solution.py:72
  20.0 0.0 copy-start.16
  20.0 0.0 copy-start.8
  20.0 0.0 copy-start.11
  20.0 4.7 %all-to-all-start.1 = ((bf16[16,4,128,256]{3,2,1,0:T(8,128)(2,1)}), bf16[16,4,128,256]{3,2,1,0:T(8,128)(2,1)}, u32[]{:S(2)}, u32[]{:S(2)}) async-start(bf16[16,4,128,256]{3,2,1,0:T(8,128)(2,1)} %bitcast.87), calls=%async_computation.1 | async-start | bytes 8388608 | tf_op jit(solution)/shard_map/all_to_all | solution.py:312
  24.7 0.0 copy-start
  24.7 0.6 broadcast_compare_fusion
  25.3 1.1 eq.49
  26.4 1.3 and.58
  27.7 0.7 fusion.6
  28.4 0.6 copy_bitcast_fusion
  29.0 1.9 reduce-window.6
  30.9 1.5 slice_reduce_fusion
  32.3 1.3 reduce-window.9
  33.6 0.7 slice.32
  34.3 0.8 bitcast_bitcast_fusion
  35.1 1.3 fusion.4
  36.4 1.3 reshape.139
  37.7 1.3 fusion.7
  39.0 1.3 eq.56
  40.3 1.0 copy-done.9
  41.3 25.3 %blocks.1 = (bf16[48,128,512]{2,1,0:T(8,128)(2,1)S(1)}, bf16[48,4,128,128]{3,2,1,0:T(8,128)(2,1)S(1)}) custom-call(s32[16,6144]{1,0:T(8,128)S(1)} %copy-done.8, s32[16,6144]{1,0:T(8,128)S(1)} %copy-done.9), custom_call_target="tpu_custom_call" | custom-call | tf_op jit(solution)/shard_map/blocks/pallas_call | solution.py:108
  66.7 2.6 %copy-done.1 = bf16[48,4,128,128]{3,2,1,0:T(8,128)(2,1)} copy-done((bf16[48,4,128,128]{3,2,1,0:T(8,128)(2,1)}, bf16[48,4,128,128]{3,2,1,0:T(8,128)(2,1)S(1)}, u32[]{:S(2)}) %copy-start.1) | copy-done | bytes 6291480
  69.3 2.6 copy-done.4
  71.9 0.8 select_reduce_fusion
  72.7 4.9 %gather_fusion = bf16[64,128,128]{2,1,0:T(8,128)(2,1)} fusion(bf16[192,128,128]{2,1,0:T(8,128)(2,1)} %bitcast.82, s32[1024]{0:T(1024)S(1)} %pad_clamp_fusion), kind=kCustom, calls=%fused_computation | custom fusion | bytes 4194560 | tf_op jit(solution)/shard_map/gather | solution.py:380
  77.7 24.5 %all-to-all-done.1 = bf16[16,4,128,256]{3,2,1,0:T(8,128)(2,1)} async-done(((bf16[16,4,128,256]{3,2,1,0:T(8,128)(2,1)}), bf16[16,4,128,256]{3,2,1,0:T(8,128)(2,1)}, u32[]{:S(2)}, u32[]{:S(2)}) %all-to-all-start.1) | async-done | bytes 4194336 | tf_op jit(solution)/shard_map/all_to_all | solution.py:312
  102.2 0.0 copy-start.3
  102.2 1.6 copy-done.3
  103.8 2.8 %copy-done.5 = bf16[48,128,512]{2,1,0:T(8,128)(2,1)S(1)} copy-done((bf16[48,128,512]{2,1,0:T(8,128)(2,1)S(1)}, bf16[48,128,512]{2,1,0:T(8,128)(2,1)}, u32[]{:S(2)}) %copy-start.5) | copy-done | bytes 6291480
  106.6 1.9 copy-done.7
  108.5 13.4 %middle.1 = (bf16[48,128,256]{2,1,0:T(8,128)(2,1)}, bf16[48,128,256]{2,1,0:T(8,128)(2,1)}, bf16[48,128,256]{2,1,0:T(8,128)(2,1)}, bf16[48,128,256]{2,1,0:T(8,128)(2,1)}, bf16[64,128,256]{2,1,0:T(8,128)(2,1)}) custom-call(s32[4,48]{1,0:T(4,128)S(1)} %get-tuple-element.50.rows_index.target_ref, s32[64]{0:T(128)S(1)} %and_select_fusion.1.term_tile, ...), custom_call_target="tpu_custom_call" | custom-call | tf_op jit(solution)/shard_map/middle/pallas_call | solution.py:211
  121.9 19.9 %all-to-all-start.2 = ((bf16[16,4,128,256]{3,2,1,0:T(8,128)(2,1)}), bf16[16,4,128,256]{3,2,1,0:T(8,128)(2,1)}, u32[]{:S(2)}, u32[]{:S(2)}) async-start(bf16[16,4,128,256]{3,2,1,0:T(8,128)(2,1)} %bitcast.86), calls=%async_computation.2 | async-start | bytes 8388608 | tf_op jit(solution)/shard_map/all_to_all | solution.py:312
  141.9 0.8 convert_reduce_fusion
  142.7 1.0 copy-done.13
  143.8 3.0 %convolution_bitcast_fusion = f32[256,256]{1,0:T(8,128)S(1)} fusion(bf16[48,128,256]{2,1,0:T(8,128)(2,1)} %get-tuple-element.36, bf16[48,128,256]{2,1,0:T(8,128)(2,1)S(1)} %copy-done.13), kind=kOutput, calls=%fused_computation.2 | convolution fusion | flops 805306368 | bytes 6553600 | tf_op jit(solution)/shard_map/dot_general | solution.py:391
  146.8 0.7 slice_select_fusion
  147.5 0.3 collective-permute-start
  147.9 1.4 collective-permute-done
  149.3 1.0 select_add_fusion
  150.3 0.0 copy-start.14
  150.3 0.7 copy-done.14
  151.0 1.9 collective-permute-start.1
  152.9 2.8 %copy-done.2 = bf16[48,4,128,128]{3,2,1,0:T(8,128)(2,1)S(1)} copy-done((bf16[48,4,128,128]{3,2,1,0:T(8,128)(2,1)S(1)}, bf16[48,4,128,128]{3,2,1,0:T(8,128)(2,1)}, u32[]{:S(2)}) %copy-start.2) | copy-done | bytes 6291480
  155.7 27.8 %local_terms.1.local_ref = f32[48,128,256]{2,1,0:T(8,128)} custom-call(s32[4,48]{1,0:T(4,128)S(1)} %get-tuple-element.50.rows_index.target_ref, bf16[48,4,128,128]{3,2,1,0:T(8,128)(2,1)S(1)} %copy-done.2, bf16[48,128,256]{2,1,0:T(8,128)(2,1)S(1)} %copy-done.6), custom_call_target="tpu_custom_call" | custom-call | tf_op jit(solution)/shard_map/local_terms/pallas_call | solution.py:255
  183.6 0.1 collective-permute-start.2
  183.7 3.6 %collective-permute-start.3 = (f32[24,256]{1,0:T(8,128)S(1)}, f32[24,256]{1,0:T(8,128)S(1)}, u32[]{:S(2)}, u32[]{:S(2)}) collective-permute-start(f32[24,256]{1,0:T(8,128)S(1)} %get-tuple-element.58), channel_id=1, source_target_pairs={{0,8},{1,9},{2,10},{3,11},{4,12},{5,13},{6,14},{7,15},{8,0},{9,1},... | collective-permute-start | bytes 73736 | tf_op jit(solution)/shard_map/ppermute | solution.py:320
  187.4 0.9 collective-permute-start.4
  188.2 22.9 %collective-permute-done.2 = f32[24,256]{1,0:T(8,128)S(1)} collective-permute-done((f32[24,256]{1,0:T(8,128)S(1)}, f32[24,256]{1,0:T(8,128)S(1)}, u32[]{:S(2)}, u32[]{:S(2)}) %collective-permute-start.2) | collective-permute-done | bytes 24608 | tf_op jit(solution)/shard_map/ppermute | solution.py:320
  211.2 26.5 %collective-permute-done.3 = f32[24,256]{1,0:T(8,128)S(1)} collective-permute-done((f32[24,256]{1,0:T(8,128)S(1)}, f32[24,256]{1,0:T(8,128)S(1)}, u32[]{:S(2)}, u32[]{:S(2)}) %collective-permute-start.3) | collective-permute-done | bytes 24608 | tf_op jit(solution)/shard_map/ppermute | solution.py:320
  237.7 0.9 collective-permute-start.5
  238.6 1.2 collective-permute-start.6
  239.8 2.4 collective-permute-start.7
  242.1 7.8 %final_sum.1 = bf16[48,128,256]{2,1,0:T(8,128)(2,1)} custom-call(s32[16,128]{1,0:T(8,128)S(1)} %get-tuple-element.30.wanted_ref, f32[48,128,256]{2,1,0:T(8,128)} %local_terms.1.local_ref, bf16[64,128,256]{2,1,0:T(8,128)(2,1)} %bitcast.14.returned_ref), custom_call_target="tpu_custom_call" | custom-call | tf_op jit(solution)/shard_map/final_sum/pallas_call | solution.py:294
  250.1 1.5 collective-permute-start.8
  251.7 3.2 %collective-permute-done.8 = f32[96,256]{1,0:T(8,128)S(1)} collective-permute-done((f32[96,256]{1,0:T(8,128)S(1)}, f32[96,256]{1,0:T(8,128)S(1)}, u32[]{:S(2)}, u32[]{:S(2)}) %collective-permute-start.8) | collective-permute-done | bytes 98336 | tf_op jit(solution)/shard_map/ppermute | solution.py:320
  254.9 0.1 collective-permute-start.9
  255.0 1.4 collective-permute-done.9
  256.5 0.7 slice.47
  257.2 0.6 slice.48
  (47 shorter events, 0.3 us)
Async XLA Ops:
  2.0 13.9 %all-to-all-start = ((s32[16,1,192]{2,1,0:T(1,128)}), s32[16,1,192]{2,1,0:T(1,128)S(1)}, u32[]{:S(2)}, u32[]{:S(2)}) async-start(s32[16,1,192]{2,1,0:T(1,128)} %broadcast_in_dim.11), calls=%async_computation | async-start | bytes 32768 | tf_op jit(solution)/shard_map/all_to_all | solution.py:352
  20.0 4.7 %copy-start.16 = (s32[4,48]{1,0:T(4,128)S(1)}, s32[4,48]{1,0:T(4,128)}, u32[]{:S(2)}) copy-start(s32[4,48]{1,0:T(4,128)} %param.10) | copy-start | bytes 2308
  20.0 20.3 %copy-start.8 = (s32[16,6144]{1,0:T(8,128)S(1)}, s32[16,6144]{1,0:T(8,128)}, u32[]{:S(2)}) copy-start(s32[16,6144]{1,0:T(8,128)} %nbr_ref) | copy-start | bytes 1179652
  20.0 82.2 %copy-start.11 = (f32[256]{0:T(256)S(1)}, f32[256]{0:T(256)}, u32[]{:S(2)}) copy-start(f32[256]{0:T(256)} %param.9) | copy-start | bytes 3076
  20.0 82.2 %all-to-all-start.1 = ((bf16[16,4,128,256]{3,2,1,0:T(8,128)(2,1)}), bf16[16,4,128,256]{3,2,1,0:T(8,128)(2,1)}, u32[]{:S(2)}, u32[]{:S(2)}) async-start(bf16[16,4,128,256]{3,2,1,0:T(8,128)(2,1)} %bitcast.87), calls=%async_computation.1 | async-start | bytes 8388608 | tf_op jit(solution)/shard_map/all_to_all | solution.py:312
  24.7 77.5 %copy-start = (bf16[6144,256]{1,0:T(8,128)(2,1)S(1)}, bf16[6144,256]{1,0:T(8,128)(2,1)}, u32[]{:S(2)}) copy-start(bf16[6144,256]{1,0:T(8,128)(2,1)} %param.7) | copy-start | bytes 9437188
  40.3 1.0 copy-start.9
  66.6 2.6 %copy-start.1 = (bf16[48,4,128,128]{3,2,1,0:T(8,128)(2,1)}, bf16[48,4,128,128]{3,2,1,0:T(8,128)(2,1)S(1)}, u32[]{:S(2)}) copy-start(bf16[48,4,128,128]{3,2,1,0:T(8,128)(2,1)S(1)} %get-tuple-element.28.columns_ref) | copy-start | bytes 18874372
  69.3 2.6 copy-start.4
  71.9 30.3 %copy-start.10 = (bf16[256,256]{1,0:T(8,128)(2,1)S(1)}, bf16[256,256]{1,0:T(8,128)(2,1)}, u32[]{:S(2)}) copy-start(bf16[256,256]{1,0:T(8,128)(2,1)} %weight_ref.1) | copy-start | bytes 393220
  102.2 1.6 copy-start.3
  103.8 2.8 %copy-start.5 = (bf16[48,128,512]{2,1,0:T(8,128)(2,1)S(1)}, bf16[48,128,512]{2,1,0:T(8,128)(2,1)}, u32[]{:S(2)}) copy-start(bf16[48,128,512]{2,1,0:T(8,128)(2,1)} %copy-done.4) | copy-start | bytes 18874372
  106.6 1.9 copy-start.7
  121.9 20.0 %copy-start.12 = (bf16[48,128,256]{2,1,0:T(8,128)(2,1)S(1)}, bf16[48,128,256]{2,1,0:T(8,128)(2,1)}, u32[]{:S(2)}) copy-start(bf16[48,128,256]{2,1,0:T(8,128)(2,1)} %get-tuple-element.37) | copy-start | bytes 9437188
  121.9 120.2 %all-to-all-start.2 = ((bf16[16,4,128,256]{3,2,1,0:T(8,128)(2,1)}), bf16[16,4,128,256]{3,2,1,0:T(8,128)(2,1)}, u32[]{:S(2)}, u32[]{:S(2)}) async-start(bf16[16,4,128,256]{3,2,1,0:T(8,128)(2,1)} %bitcast.86), calls=%async_computation.2 | async-start | bytes 8388608 | tf_op jit(solution)/shard_map/all_to_all | solution.py:312
  141.9 1.9 copy-start.13
  143.7 9.2 %copy-start.6 = (bf16[48,128,256]{2,1,0:T(8,128)(2,1)S(1)}, bf16[48,128,256]{2,1,0:T(8,128)(2,1)}, u32[]{:S(2)}) copy-start(bf16[48,128,256]{2,1,0:T(8,128)(2,1)} %get-tuple-element.35.grad_ref) | copy-start | bytes 9437188
  147.5 1.8 collective-permute-start
  150.3 0.7 copy-start.14
  151.0 32.6 %collective-permute-start.1 = (f32[96,256]{1,0:T(8,128)S(1)}, f32[96,256]{1,0:T(8,128)S(1)}, u32[]{:S(2)}, u32[]{:S(2)}) collective-permute-start(f32[96,256]{1,0:T(8,128)S(1)} %slice_select_fusion.1), channel_id=1, source_target_pairs={{0,2},{1,3},{2,0},{3,1},{4,6},{5,7},{6,4},{7,5},{8,10},{9,11},{10,... | collective-permute-start | bytes 294920 | tf_op jit(solution)/shard_map/ppermute | solution.py:320
  152.9 2.8 %copy-start.2 = (bf16[48,4,128,128]{3,2,1,0:T(8,128)(2,1)S(1)}, bf16[48,4,128,128]{3,2,1,0:T(8,128)(2,1)}, u32[]{:S(2)}) copy-start(bf16[48,4,128,128]{3,2,1,0:T(8,128)(2,1)} %copy-done.1) | copy-start | bytes 18874372
  155.7 27.8 %copy-start.15 = (f32[192,256]{1,0:T(8,128)S(1)}, f32[192,256]{1,0:T(8,128)}, u32[]{:S(2)}) copy-start(f32[192,256]{1,0:T(8,128)} %copy-done.14) | copy-start | bytes 589828
  183.6 27.6 %collective-permute-start.2 = (f32[24,256]{1,0:T(8,128)S(1)}, f32[24,256]{1,0:T(8,128)S(1)}, u32[]{:S(2)}, u32[]{:S(2)}) collective-permute-start(f32[24,256]{1,0:T(8,128)S(1)} %get-tuple-element.56), channel_id=1, source_target_pairs={{0,4},{1,5},{2,6},{3,7},{4,0},{5,1},{6,2},{7,3},{8,12},{9,13},{10,... | collective-permute-start | bytes 73736 | tf_op jit(solution)/shard_map/ppermute | solution.py:320
  183.7 54.0 %collective-permute-start.3 = (f32[24,256]{1,0:T(8,128)S(1)}, f32[24,256]{1,0:T(8,128)S(1)}, u32[]{:S(2)}, u32[]{:S(2)}) collective-permute-start(f32[24,256]{1,0:T(8,128)S(1)} %get-tuple-element.58), channel_id=1, source_target_pairs={{0,8},{1,9},{2,10},{3,11},{4,12},{5,13},{6,14},{7,15},{8,0},{9,1},... | collective-permute-start | bytes 73736 | tf_op jit(solution)/shard_map/ppermute | solution.py:320
  187.4 50.3 %collective-permute-start.4 = (f32[24,256]{1,0:T(8,128)S(1)}, f32[24,256]{1,0:T(8,128)S(1)}, u32[]{:S(2)}, u32[]{:S(2)}) collective-permute-start(f32[24,256]{1,0:T(8,128)S(1)} %get-tuple-element.57), channel_id=1, source_target_pairs={{0,12},{1,13},{2,14},{3,15},{4,8},{5,9},{6,10},{7,11},{8,4},{9,5},... | collective-permute-start | bytes 73736 | tf_op jit(solution)/shard_map/ppermute | solution.py:320
  237.7 12.3 %collective-permute-start.5 = (f32[24,256]{1,0:T(8,128)S(1)}, f32[24,256]{1,0:T(8,128)S(1)}, u32[]{:S(2)}, u32[]{:S(2)}) collective-permute-start(f32[24,256]{1,0:T(8,128)S(1)} %fusion.2), channel_id=1, source_target_pairs={{0,4},{1,5},{2,6},{3,7},{4,0},{5,1},{6,2},{7,3},{8,12},{9,13},{10,... | collective-permute-start | bytes 73736 | tf_op jit(solution)/shard_map/ppermute | solution.py:320
  238.6 11.4 %collective-permute-start.6 = (f32[24,256]{1,0:T(8,128)S(1)}, f32[24,256]{1,0:T(8,128)S(1)}, u32[]{:S(2)}, u32[]{:S(2)}) collective-permute-start(f32[24,256]{1,0:T(8,128)S(1)} %fusion.2), channel_id=1, source_target_pairs={{0,8},{1,9},{2,10},{3,11},{4,12},{5,13},{6,14},{7,15},{8,0},{9,1},... | collective-permute-start | bytes 73736 | tf_op jit(solution)/shard_map/ppermute | solution.py:320
  239.8 10.3 %collective-permute-start.7 = (f32[24,256]{1,0:T(8,128)S(1)}, f32[24,256]{1,0:T(8,128)S(1)}, u32[]{:S(2)}, u32[]{:S(2)}) collective-permute-start(f32[24,256]{1,0:T(8,128)S(1)} %fusion.2), channel_id=1, source_target_pairs={{0,12},{1,13},{2,14},{3,15},{4,8},{5,9},{6,10},{7,11},{8,4},{9,5},... | collective-permute-start | bytes 73736 | tf_op jit(solution)/shard_map/ppermute | solution.py:320
  250.1 4.7 %collective-permute-start.8 = (f32[96,256]{1,0:T(8,128)S(1)}, f32[96,256]{1,0:T(8,128)S(1)}, u32[]{:S(2)}, u32[]{:S(2)}) collective-permute-start(f32[96,256]{1,0:T(8,128)S(1)} %pad_maximum_fusion.2), channel_id=1, source_target_pairs={{0,2},{1,3},{2,0},{3,1},{4,6},{5,7},{6,4},{7,5},{8,10},{9,11},{10,... | collective-permute-start | bytes 294920 | tf_op jit(solution)/shard_map/ppermute | solution.py:320
  254.9 1.5 collective-permute-start.9
